TPU v7x, 32 devices: a whole 2x2x4 slice. The times are simulated.
32 devices in a mesh: wide: 8 (over y, x, core), narrow: 4 (over z).
Axes of the slice: x: 2, y: 2, z: 4, core: 2. Of those that a mesh axis runs over, the one named last changes fastest.
Arguments:
- row_vectors: bfloat16 [8192, 2048], P('wide'), may hold values from -0.59765625 to 1.3984375
- col_vectors: bfloat16 [2048, 2048], P('narrow', 'wide'), may hold values from -0.59765625 to 1.3984375
- primal_matrix: bfloat16 [2048, 2048], P('wide'), may hold values from -1 to 3, as said below
- dual_inverse: bfloat16 [2048, 2048], P('wide'), may hold values from -1 to 3, as said below
Outputs:
- factored: float32 [8192, 2048], P('wide', 'narrow')
Inputs may be any that keep to these rules, and one draw needn't show every extreme that they name: `primal_matrix`: symmetric positive definite. `dual_inverse`: symmetric positive definite.
All inputs are finite; a program needn't handle non-finite values.
Results may differ from a plain program's by a relative error of at most 0.0027.
Values may be sent and summed in bfloat16 or wider, within the bound.
No kernel may reach another device: no remote copies, remote signals or barrier semaphores. Data moves between devices by JAX's collectives and lax.ppermute only.
A program may use at most 64 MiB of HBM per device.

v0:
```python
import functools

import jax
import jax.numpy as jnp
from jax import lax
from jax.experimental import pallas as pl
from jax.experimental.pallas import tpu as pltpu
from jax.sharding import PartitionSpec as P

HIGHEST = lax.Precision.HIGHEST
NN = (((1,), (0,)), ((), ()))
NT = (((1,), (1,)), ((), ()))
TN = (((0,), (0,)), ((), ()))
VMEM = pl.BlockSpec(memory_space=pltpu.VMEM)
SMEM = pl.BlockSpec(memory_space=pltpu.SMEM)


def after(value, *earlier):
    return lax.optimization_barrier((value,) + earlier)[0]


def swap(value, mask, count):
    return lax.ppermute(value, "wide", [(i, i ^ mask) for i in range(count)])


def forward(pieces, mask, count):
    high = 1 << (mask.bit_length() - 1)
    low = mask & -mask
    if high == low:
        return swap(pieces[0], mask, count)
    even = lax.axis_index("wide") % 2 == 0
    held = jnp.where(even, pieces[mask ^ high], pieces[mask ^ low])
    return lax.ppermute(held, "wide", [(i, i ^ (low if i % 2 else high)) for i in range(count)])


def gather_pieces(value, count):
    pieces = [value] + [None] * (count - 1)
    masks = sorted(range(2, count, 2), key=lambda m: (bin(m).count("1"), m))
    for mask in masks:
        pieces[mask] = forward(pieces, mask, count)
    for mask in range(1, count, 2):
        pieces[mask] = swap(pieces[mask - 1], 1, count)
    return pieces


def from_first(value):
    count = lax.axis_size("narrow")
    total = jnp.where(lax.axis_index("narrow") == 0, value, 0).astype(value.dtype)
    for target in range(1, count):
        total = total + lax.ppermute(value, "narrow", [(0, target)])
    return total


def dot(left, right, dims=NN, precision=None):
    return lax.dot_general(
        left, right, dims, precision=precision, preferred_element_type=jnp.float32
    )


def halves(value):
    high = value.astype(jnp.bfloat16)
    return high, (value - high.astype(jnp.float32)).astype(jnp.bfloat16)


def dot_halves(left, right, dims):
    left_high, left_low = left
    right_high, right_low = right
    return dot(left_high, right_high, dims) + (
        dot(left_high, right_low, dims) + dot(left_low, right_high, dims)
    )


def eliminate(block):
    size = block.shape[0]
    groups = size // 8
    rows = lax.broadcasted_iota(jnp.int32, (8, size), 0)
    lanes = lax.broadcasted_iota(jnp.int32, (8, size), 1)
    left = [block[8 * i : 8 * i + 8] for i in range(groups)]
    right = [jnp.where(lanes == rows + 8 * i, 1.0, 0.0).astype(jnp.float32) for i in range(groups)]

    def column(value, j):
        return jnp.broadcast_to(value[:, j : j + 1], (8, size))

    def row(value, i):
        return jnp.broadcast_to(value[i : i + 1, :], (8, size))

    pivots = [None] * size
    first = {i: column(left[i], 0) for i in range(groups)}
    second = {i: column(left[i], 1) for i in range(groups)}
    for j in range(0, size, 2):
        g, r = j // 8, j % 8
        top = row(first[g], r)
        side = row(first[g], r + 1)
        minor = top * row(second[g], r + 1) - side * side
        top_inverse = 1.0 / top
        factor = side * top_inverse
        low_inverse = top * (1.0 / minor)
        pivots[j] = top
        pivots[j + 1] = minor * top_inverse
        left_top = row(left[g], r)
        left_low = (row(left[g], r + 1) - factor * left_top) * low_inverse
        left_top = left_top * top_inverse
        right_top = row(right[g], r)
        right_next = row(right[g], r + 1) - factor * right_top
        right_low = right_next * low_inverse
        right_top = right_top * top_inverse
        a, b = {}, {}
        for i in range(g, groups):
            if i > g:
                a[i], b[i] = first[i], second[i] - first[i] * factor
            elif r < 6:
                below = rows > r + 1
                a[i] = jnp.where(below, first[i], 0.0)
                b[i] = jnp.where(below, second[i] - first[i] * factor, 0.0)
        if j + 2 < size:
            ahead = [{}, {}]
            for q in range(2):
                lead = column(left[g], j + 2 + q)
                high = row(lead, r)
                low = (row(lead, r + 1) - factor * high) * low_inverse
                high = high * top_inverse
                for i in range((j + 2) // 8, groups):
                    value = lead if i == g else column(left[i], j + 2 + q)
                    ahead[q][i] = value - a[i] * high - b[i] * low
            first, second = ahead
        right[g] = jnp.where(rows == r + 1, right_next, right[g])
        for i in a:
            left[i] = left[i] - a[i] * left_top - b[i] * left_low
            right[i] = right[i] - a[i] * right_top - b[i] * right_low
    out = []
    for i in range(groups):
        pivot = pivots[8 * i]
        for q in range(1, 8):
            pivot = jnp.where(rows == q, pivots[8 * i + q], pivot)
        out.append(right[i] * lax.rsqrt(pivot))
    return jnp.concatenate(out, axis=0)


def block_of(ref, me_ref, mask, size):
    if size % 128:
        return ref[:, mask * size : (mask + 1) * size]
    return ref[:, pl.ds(pl.multiple_of((me_ref[0] ^ mask) * size, size), size)]


def products_kernel(me_ref, primal_ref, dual_ref, *refs):
    pieces, out_ref = refs[:-1], refs[-1]
    size = primal_ref.shape[0]
    for which, ref in enumerate((primal_ref, dual_ref)):
        total = None
        for mask, piece in enumerate(pieces):
            part = dot(block_of(ref, me_ref, mask, size), piece[...], NT)
            total = part if total is None else total + part
        out_ref[which] = total.astype(out_ref.dtype)


def products(me, primal, dual, pieces):
    size, width = primal.shape[0], pieces[0].shape[0]
    return pl.pallas_call(
        products_kernel,
        out_shape=jax.ShapeDtypeStruct((2, size, width), jnp.bfloat16),
        in_specs=[SMEM] + [VMEM] * (2 + len(pieces)),
        out_specs=VMEM,
        name="products",
    )(me, primal, dual, *pieces)


def summed(lines, sides, which):
    total = None
    for line, side in zip(lines, sides):
        part = dot(line[...], side[which])
        total = part if total is None else total + part
    return total


def row_lines(rows, me, share, tile, masks):
    if share % 128:
        arrays = [
            lax.dynamic_slice_in_dim(rows, (me[0] ^ mask) * share, share, 1) for mask in masks
        ]
        return arrays, [pl.BlockSpec((tile, share), lambda i, s: (i, 0))] * len(masks)
    specs = [
        pl.BlockSpec((tile, share), lambda i, s, mask=mask: (i, s[0] ^ mask)) for mask in masks
    ]
    return [rows] * len(masks), specs


def piece_lines(pieces, tile, masks):
    share = pieces[0].shape[1]
    spec = pl.BlockSpec((tile, share), lambda i, s: (i, 0))
    return [pieces[mask] for mask in masks], [spec] * len(masks)


def side_specs(sides):
    return [pl.BlockSpec(side.shape, lambda i, s: (0, 0, 0)) for side in sides]


def call(kernel, steps, scalars, operands, specs, out_shape, out_spec, **more):
    scratch = more.pop("scratch_shapes", ())
    return pl.pallas_call(
        kernel,
        grid_spec=pltpu.PrefetchScalarGridSpec(
            num_scalar_prefetch=1,
            grid=(steps,),
            in_specs=specs,
            out_specs=out_spec,
            scratch_shapes=scratch,
        ),
        out_shape=out_shape,
        **more,
    )(scalars, *operands)


def accumulate_kernel(count, fresh, scalars, *refs):
    lines, sides, out_ref = refs[:count], refs[count : 2 * count], refs[-1]
    for which in range(2):
        total = summed(lines, sides, which)
        out_ref[which] = total if fresh else refs[2 * count][which] + total


def accumulate(scalars, height, tile, lines, sides, earlier=None):
    arrays, specs = lines
    width = sides[0].shape[2]
    total = pl.BlockSpec((2, tile, width), lambda i, s: (0, i, 0))
    count = len(arrays)
    more = [] if earlier is None else [earlier]
    return call(
        functools.partial(accumulate_kernel, count, earlier is None),
        height // tile,
        scalars,
        [*arrays, *sides, *more],
        specs + side_specs(sides) + [total] * len(more),
        jax.ShapeDtypeStruct((2, height, width), jnp.float32),
        total,
        input_output_aliases={2 * count + 1: 0} if more else {},
    )


def inverse_kernel(size, scale, count, scalars, *refs):
    lines, sides = refs[:count], refs[count : 2 * count]
    total_ref, out_ref, work, line = refs[2 * count :]
    order = out_ref.shape[1]
    gram = (
        (total_ref[0] + summed(lines, sides, 0)) * (total_ref[1] + summed(lines, sides, 1)) * scale
    )
    work[:, :order] = (gram + gram.T) * 0.5
    work[:, order:] = jnp.where(
        lax.broadcasted_iota(jnp.int32, (order, order), 0)
        == lax.broadcasted_iota(jnp.int32, (order, order), 1),
        1.0,
        0.0,
    ).astype(jnp.float32)
    for start in range(0, order, size):
        stop = start + size
        inverse = eliminate(work[start:stop, start:stop])
        line[:, start : order + stop] = dot(
            inverse, work[start:stop, start : order + stop], NN, HIGHEST
        )
        out_ref[0, start:stop, :stop], out_ref[1, start:stop, :stop] = halves(
            line[:, order : order + stop]
        )
        if stop < order:
            out_ref[:, start:stop, stop:] = jnp.zeros((2, size, order - stop), out_ref.dtype)
            work[stop:, stop : order + stop] -= dot(
                line[:, stop:order], line[:, stop : order + stop], TN, HIGHEST
            )


def factor_inverse(scalars, total, lines, sides, scale):
    size = 128
    arrays, specs = lines
    order = sides[0].shape[2]
    return call(
        functools.partial(inverse_kernel, size, scale, len(arrays)),
        1,
        scalars,
        [*arrays, *sides, total],
        specs + side_specs(sides + [total]),
        jax.ShapeDtypeStruct((2, order, order), jnp.bfloat16),
        pl.BlockSpec((2, order, order), lambda i, s: (0, 0, 0)),
        scratch_shapes=[
            pltpu.VMEM((order, 2 * order), jnp.float32),
            pltpu.VMEM((size, 2 * order), jnp.float32),
        ],
        cost_estimate=pl.CostEstimate(
            flops=15_000_000_000, transcendentals=order, bytes_accessed=8 * order * order
        ),
    )


def project_kernel(scale, count, fresh, scalars, *refs):
    lines, sides = refs[:count], refs[count : 2 * count]
    inverse_ref, out_ref = refs[2 * count], refs[-1]
    parts = [summed(lines, sides, which) for which in range(2)]
    if not fresh:
        parts = [part + refs[2 * count + 1][which] for which, part in enumerate(parts)]
    left = halves(parts[0] * parts[1] * scale)
    half = inverse_ref.shape[1] // 2
    low = dot_halves(
        [v[:, :half] for v in left], [inverse_ref[q, :half, :half] for q in range(2)], NT
    )
    high = dot_halves(left, [inverse_ref[q, half:, :] for q in range(2)], NT)
    if len(out_ref.shape) == 2:
        out_ref[:, :half] = low
        out_ref[:, half:] = high
    else:
        out_ref[0, :, :half], out_ref[1, :, :half] = halves(low)
        out_ref[0, :, half:], out_ref[1, :, half:] = halves(high)


def project(scalars, height, tile, lines, sides, inverse, scale, split, earlier=None):
    arrays, specs = lines
    width = sides[0].shape[2]
    count = len(arrays)
    both = pl.BlockSpec((2, tile, width), lambda i, s: (0, i, 0))
    more = [] if earlier is None else [earlier]
    if split:
        out = jax.ShapeDtypeStruct((2, height, width), jnp.bfloat16), both
    else:
        out = (
            jax.ShapeDtypeStruct((height, width), jnp.float32),
            pl.BlockSpec((tile, width), lambda i, s: (i, 0)),
        )
    return call(
        functools.partial(project_kernel, scale, count, earlier is None),
        height // tile,
        scalars,
        [*arrays, *sides, inverse, *more],
        specs + side_specs(sides + [inverse]) + [both] * len(more),
        *out,
    )


def update_kernel(scale, count, scalars, *refs):
    lines, sides = refs[:count], refs[count : 2 * count]
    panel_ref, solved_ref, out_ref = refs[2 * count :]
    slab = summed(lines, sides, 0) * summed(lines, sides, 1) * scale
    panel = panel_ref[...]
    trailing = slab - dot_halves(halves(panel), [solved_ref[q] for q in range(2)], NT)
    out_ref[...] = jnp.where(scalars[1] == 0, panel, trailing)


def update(scalars, height, tile, lines, sides, panel, solved, scale):
    arrays, specs = lines
    width = sides[0].shape[2]
    tiles = pl.BlockSpec((tile, width), lambda i, s: (i, 0))
    return call(
        functools.partial(update_kernel, scale, len(arrays)),
        height // tile,
        scalars,
        [*arrays, *sides, panel, solved],
        specs + side_specs(sides) + [tiles] + side_specs([solved]),
        jax.ShapeDtypeStruct((height, width), jnp.float32),
        tiles,
    )


def per_device(row_vectors, col_vectors, primal_matrix, dual_inverse):
    count = lax.axis_size("wide")
    me = lax.axis_index("wide")
    share, cone_order = primal_matrix.shape
    height = row_vectors.shape[0]
    order = col_vectors.shape[0]
    tile = 256
    scale = 16.0 / (cone_order * cone_order)
    scalars = jnp.stack([me, lax.axis_index("narrow")]).astype(jnp.int32)
    early, late, every = range(2, count - 2), range(count - 2, count), range(count)

    if share % 128:
        primal_matrix, dual_inverse = (
            jnp.concatenate(
                [
                    lax.dynamic_slice_in_dim(value, (me ^ mask) * share, share, 1)
                    for mask in every
                ],
                axis=1,
            )
            for value in (primal_matrix, dual_inverse)
        )

    def rows(masks):
        return row_lines(row_vectors, scalars, share, tile, masks)

    panel = from_first(col_vectors)
    columns = gather_pieces(col_vectors, count)
    panel = after(panel, *columns)
    own = products(scalars, primal_matrix, dual_inverse, columns)
    panels = gather_pieces(panel, count)
    first = products(scalars, primal_matrix, dual_inverse, [after(panels[0], own), *panels[1:]])

    masks = sorted(range(2, count, 2), key=lambda m: (bin(m).count("1"), m))
    firsts = [first] + [None] * (count - 1)
    firsts[1] = swap(first, 1, count)
    begun = False
    for mask in masks:
        if bin(mask).count("1") > 1 and not begun:
            begun = True
            start = accumulate(scalars, height, tile, rows((0, 1)), firsts[:2])
            for bit in masks:
                if bin(bit).count("1") == 1:
                    firsts[bit] = after(firsts[bit], start)
                    firsts[bit + 1] = swap(firsts[bit], 1, count)
        firsts[mask] = forward(firsts, mask, count)
    for mask in masks:
        if firsts[mask + 1] is None and mask != count - 2:
            firsts[mask + 1] = swap(firsts[mask], 1, count)
    total = accumulate(
        scalars, order, tile, piece_lines(panels, tile, range(count - 2)), firsts[:-2]
    )
    middle = accumulate(scalars, height, tile, rows(early), firsts[2:-2], start)
    firsts[-2] = after(firsts[-2], total, middle)
    firsts[-1] = swap(firsts[-2], 1, count)

    owns = [own] + [None] * (count - 1)
    delayed = after(own, firsts[-2])
    for mask in range(2, count, 2):
        owns[mask] = swap(delayed, mask, count)
    owns[1] = swap(delayed, 1, count)
    inverse = factor_inverse(scalars, total, piece_lines(panels, order, late), firsts[-2:], scale)
    for mask in range(2, count, 2):
        owns[mask + 1] = swap(after(owns[mask], inverse), 1, count)

    solved = project(
        scalars, order, tile, piece_lines(columns, tile, every), firsts, inverse, scale, True
    )
    panel_cols = project(
        scalars, height, tile, rows(late), firsts[-2:], inverse, scale, False, middle
    )
    return update(scalars, height, tile, rows(every), owns, panel_cols, solved, scale)


def solution(mesh):
    placed = (P("wide", None), P("narrow", "wide"), P("wide", None), P("wide", None))
    return jax.shard_map(
        per_device, mesh=mesh, in_specs=placed, out_specs=P("wide", "narrow"), check_vma=False
    )
```

profile of v0, /device:TPU:0, one launch (start us, length us, event | category | flops | bytes accessed | tf_op | source)
XLA Modules:
  0.0 144.7 jit_solution(4514091401363808210)
XLA Ops:
  0.0 3.0 %collective-permute-start.1 = (bf16[512,256]{1,0:T(8,128)(2,1)}, bf16[512,256]{1,0:T(8,128)(2,1)S(1)}, u32[]{:S(2)}, u32[]{:S(2)}) collective-permute-start(bf16[512,256]{1,0:T(8,128)(2,1)} %refs_0_.10), channel_id=1, source_target_pairs={{0,8},{4,12},{8,0},{12,4},{16,24},{20,28},{24,16},{28,20},{1,9},{5... | collective-permute-start | bytes 786440 | tf_op jit(solution)/shard_map/ppermute | solution.py:23
  3.0 1.5 %collective-permute-start.3 = (bf16[512,256]{1,0:T(8,128)(2,1)}, bf16[512,256]{1,0:T(8,128)(2,1)S(1)}, u32[]{:S(2)}, u32[]{:S(2)}) collective-permute-start(bf16[512,256]{1,0:T(8,128)(2,1)} %refs_0_.10), channel_id=1, source_target_pairs={{0,16},{4,20},{8,24},{12,28},{16,0},{20,4},{24,8},{28,12},{1,17},{... | collective-permute-start | bytes 786440 | tf_op jit(solution)/shard_map/ppermute | solution.py:23
  4.5 3.5 %collective-permute-start.7 = (bf16[512,256]{1,0:T(8,128)(2,1)}, bf16[512,256]{1,0:T(8,128)(2,1)S(1)}, u32[]{:S(2)}, u32[]{:S(2)}) collective-permute-start(bf16[512,256]{1,0:T(8,128)(2,1)} %refs_0_.10), channel_id=1, source_target_pairs={{0,1},{4,5},{8,9},{12,13},{16,17},{20,21},{24,25},{28,29}} | collective-permute-start | bytes 786440 | tf_op jit(solution)/shard_map/ppermute | solution.py:50
  8.0 1.7 %collective-permute-start.8 = (bf16[512,256]{1,0:T(8,128)(2,1)}, bf16[512,256]{1,0:T(8,128)(2,1)S(1)}, u32[]{:S(2)}, u32[]{:S(2)}) collective-permute-start(bf16[512,256]{1,0:T(8,128)(2,1)} %refs_0_.10), channel_id=1, source_target_pairs={{0,2},{4,6},{8,10},{12,14},{16,18},{20,22},{24,26},{28,30}} | collective-permute-start | bytes 786440 | tf_op jit(solution)/shard_map/ppermute | solution.py:50
  9.7 1.2 collective-permute-done.3.refs_4_
  11.0 1.6 %collective-permute-start.5 = (bf16[512,256]{1,0:T(8,128)(2,1)S(1)}, bf16[512,256]{1,0:T(8,128)(2,1)S(1)}, u32[]{:S(2)}, u32[]{:S(2)}) collective-permute-start(bf16[512,256]{1,0:T(8,128)(2,1)S(1)} %broadcast_select_fusion.2), channel_id=1, source_target_pairs={{0,16},{4,12},{8,24},{12,4},{16,0},{20,28},{24,8},{28,20},{1,17},{... | collective-permute-start | bytes 786440 | tf_op jit(solution)/shard_map/ppermute | solution.py:33
  12.6 5.5 %collective-permute-start.9 = (bf16[512,256]{1,0:T(8,128)(2,1)}, bf16[512,256]{1,0:T(8,128)(2,1)S(1)}, u32[]{:S(2)}, u32[]{:S(2)}) collective-permute-start(bf16[512,256]{1,0:T(8,128)(2,1)} %refs_0_.10), channel_id=1, source_target_pairs={{0,3},{4,7},{8,11},{12,15},{16,19},{20,23},{24,27},{28,31}} | collective-permute-start | bytes 786440 | tf_op jit(solution)/shard_map/ppermute | solution.py:50
  18.1 0.1 collective-permute-start
  18.2 0.0 collective-permute-done.7
  18.2 0.5 collective-permute-start.2
  18.7 1.9 %collective-permute-done.8 = bf16[512,256]{1,0:T(8,128)(2,1)S(1)} collective-permute-done((bf16[512,256]{1,0:T(8,128)(2,1)}, bf16[512,256]{1,0:T(8,128)(2,1)S(1)}, u32[]{:S(2)}, u32[]{:S(2)}) %collective-permute-start.8) | collective-permute-done | bytes 262176 | tf_op jit(solution)/shard_map/ppermute | solution.py:50
  20.6 0.0 collective-permute-start.4
  20.6 0.0 collective-permute-done.5.refs_6_
  20.6 0.5 collective-permute-start.6
  21.1 3.4 %collective-permute-done.9 = bf16[512,256]{1,0:T(8,128)(2,1)S(1)} collective-permute-done((bf16[512,256]{1,0:T(8,128)(2,1)}, bf16[512,256]{1,0:T(8,128)(2,1)S(1)}, u32[]{:S(2)}, u32[]{:S(2)}) %collective-permute-start.9) | collective-permute-done | bytes 262176 | tf_op jit(solution)/shard_map/ppermute | solution.py:50
  24.5 1.0 add_add_fusion.refs_0_
  25.5 0.0 collective-permute-done.refs_1_
  25.6 0.0 collective-permute-done.4.refs_5_
  25.6 0.0 collective-permute-done.6.refs_7_
  25.6 0.6 collective-permute-start.11
  26.2 0.5 collective-permute-start.13
  26.7 5.6 %collective-permute-done.11.refs_2_ = bf16[512,256]{1,0:T(8,128)(2,1)S(1)} collective-permute-done((bf16[512,256]{1,0:T(8,128)(2,1)S(1)}, bf16[512,256]{1,0:T(8,128)(2,1)S(1)}, u32[]{:S(2)}, u32[]{:S(2)}) %collective-permute-start.11) | collective-permute-done | bytes 262176 | tf_op jit(solution)/shard_map/ppermute | solution.py:23
  32.3 0.3 collective-permute-done.13.refs_4_
  32.6 1.2 collective-permute-start.15
  33.9 0.5 collective-permute-start.12
  34.4 0.0 collective-permute-start.14
  34.4 4.8 %collective-permute-done.15.refs_6_.refs_0_ = bf16[512,256]{1,0:T(8,128)(2,1)} collective-permute-done((bf16[512,256]{1,0:T(8,128)(2,1)S(1)}, bf16[512,256]{1,0:T(8,128)(2,1)}, u32[]{:S(2)}, u32[]{:S(2)}) %collective-permute-start.15) | collective-permute-done | bytes 262176 | tf_op jit(solution)/shard_map/ppermute | solution.py:33
  39.2 0.0 collective-permute-start.16
  39.2 0.6 pad_add_fusion.me_ref.scalars
  39.8 4.2 %products.2.refs_8_ = bf16[2,256,512]{2,1,0:T(8,128)(2,1)} custom-call(s32[2]{0:T(128)} %pad_add_fusion.me_ref.scalars, bf16[256,2048]{1,0:T(8,128)(2,1)} %primal_ref.3, bf16[256,2048]{1,0:T(8,128)(2,1)} %dual_ref.3, bf16[512,256]{1,0:T(8,128)(2,1)} %refs_0_.10, bf16[512,256]{1,0:T(8,128)(2,1)} %copy-done.14, bf16[512,256]{1,0:T(8,128)(2,1)} %copy-done.6, ...), custom_call_target="tpu_custom_call" | custom-call | tf_op jit(solution)/shard_map/products/pallas_call | solution.py:158
  44.0 0.0 collective-permute-done.10.refs_1_
  44.1 0.0 collective-permute-done.12.refs_3_
  44.1 0.6 copy-done.18
  44.7 0.2 copy-done.19
  44.9 0.1 copy-done.20
  45.0 4.2 %products.3.refs_2_.refs_6_.refs_8_ = bf16[2,256,512]{2,1,0:T(8,128)(2,1)} custom-call(s32[2]{0:T(128)} %pad_add_fusion.me_ref.scalars, bf16[256,2048]{1,0:T(8,128)(2,1)} %primal_ref.3, bf16[256,2048]{1,0:T(8,128)(2,1)} %dual_ref.3, bf16[512,256]{1,0:T(8,128)(2,1)} %copy-done.5, bf16[512,256]{1,0:T(8,128)(2,1)} %copy-done.18, bf16[512,256]{1,0:T(8,128)(2,1)} %copy-done.8, ...), custom_call_target="tpu_custom_call" | custom-call | tf_op jit(solution)/shard_map/products/pallas_call | solution.py:158
  49.3 0.5 collective-permute-start.18
  49.8 1.2 collective-permute-start.19
  50.9 0.8 collective-permute-start.17
  51.8 0.8 copy-done.4
  52.6 5.9 %shard_map.46.refs_8_ = f32[2,1024,512]{2,1,0:T(8,128)} custom-call(s32[2]{0:T(128)} %pad_add_fusion.me_ref.scalars, bf16[1024,2048]{1,0:T(8,128)(2,1)} %refs_7_.1, bf16[1024,2048]{1,0:T(8,128)(2,1)} %refs_7_.1, bf16[2,256,512]{2,1,0:T(8,128)(2,1)} %products.3.refs_2_.refs_6_.refs_8_, bf16[2,256,512]{2,1,0:T(8,128)(2,1)} %copy-done.4), custom_call_target="tpu_custom_call" | custom-call | tf_op jit(solution)/shard_map/pallas_call | solution.py:199
  58.5 5.3 %collective-permute-done.19.refs_10_.refs_6_.refs_12_ = bf16[2,256,512]{2,1,0:T(8,128)(2,1)S(1)} collective-permute-done((bf16[2,256,512]{2,1,0:T(8,128)(2,1)}, bf16[2,256,512]{2,1,0:T(8,128)(2,1)S(1)}, u32[]{:S(2)}, u32[]{:S(2)}) %collective-permute-start.19) | collective-permute-done | bytes 524320 | tf_op jit(solution)/shard_map/ppermute | solution.py:23
  63.8 0.9 collective-permute-done.17.refs_8_.refs_4_.refs_10_
  64.7 0.1 broadcast_select_fusion
  64.8 0.9 collective-permute-start.20
  65.7 0.0 collective-permute-done.22.refs_11_.refs_7_.refs_13_
  65.7 0.9 collective-permute-done.21.refs_9_.refs_5_.refs_11_
  66.6 0.8 copy-done.3
  67.4 8.2 %shard_map.48.refs_5_ = f32[2,1024,512]{2,1,0:T(8,128)} custom-call(s32[2]{0:T(128)} %pad_add_fusion.me_ref.scalars, bf16[1024,2048]{1,0:T(8,128)(2,1)} %refs_7_.1, bf16[1024,2048]{1,0:T(8,128)(2,1)} %refs_7_.1, bf16[1024,2048]{1,0:T(8,128)(2,1)} %refs_7_.1, bf16[1024,2048]{1,0:T(8,128)(2,1)} %refs_7_.1, ...), custom_call_target="tpu_custom_call", output_to_operand_aliasing={{}: (9, {})} | custom-call | tf_op jit(solution)/shard_map/pallas_call | solution.py:199
  75.7 6.1 %shard_map.47.refs_4_ = f32[2,512,512]{2,1,0:T(8,128)} custom-call(s32[2]{0:T(128)} %pad_add_fusion.me_ref.scalars, bf16[512,256]{1,0:T(8,128)(2,1)} %copy-done.5, bf16[512,256]{1,0:T(8,128)(2,1)} %copy-done.18, bf16[512,256]{1,0:T(8,128)(2,1)} %copy-done.8, bf16[512,256]{1,0:T(8,128)(2,1)} %copy-done.19, bf16[512,256]{1,0:T(8,128)(2,1)} %copy-done.9, ...), custom_call_target="tpu_custom_call" | custom-call | tf_op jit(solution)/shard_map/pallas_call | solution.py:199
  81.8 0.2 collective-permute-start.25
  82.0 1.8 %collective-permute-start.29 = (bf16[2,256,512]{2,1,0:T(8,128)(2,1)S(1)}, bf16[2,256,512]{2,1,0:T(8,128)(2,1)S(1)}, u32[]{:S(2)}, u32[]{:S(2)}) collective-permute-start(bf16[2,256,512]{2,1,0:T(8,128)(2,1)S(1)} %copy-done.10), channel_id=1, source_target_pairs={{0,24},{4,28},{8,16},{12,20},{16,8},{20,12},{24,0},{28,4},{1,25},{... | collective-permute-start | bytes 1572872 | tf_op jit(solution)/shard_map/ppermute | solution.py:23
  83.8 1.1 collective-permute-start.27
  84.8 0.6 collective-permute-start.24
  85.5 0.8 copy-done.12
  86.3 27.8 %shard_map.49.refs_4_.refs_16_ = bf16[2,512,512]{2,1,0:T(8,128)(2,1)} custom-call(s32[2]{0:T(128)} %pad_add_fusion.me_ref.scalars, bf16[512,256]{1,0:T(8,128)(2,1)} %collective-permute-done.15.refs_6_.refs_0_, bf16[512,256]{1,0:T(8,128)(2,1)} %collective-permute-done.16.refs_7_.refs_1_, bf16[2,256,512]{2,1,0:T(8,128)(2,1)} %copy-done.11, ...), custom_call_target="tpu_custom_call" | custom-call | flops 15000000512 | bytes 2097152 | tf_op jit(solution)/shard_map/pallas_call | solution.py:199
  114.1 0.5 collective-permute-start.30
  114.6 0.1 collective-permute-start.28
  114.7 0.4 collective-permute-start.26
  115.1 8.3 %shard_map.51.refs_17_ = bf16[2,512,512]{2,1,0:T(8,128)(2,1)} custom-call(s32[2]{0:T(128)} %pad_add_fusion.me_ref.scalars, bf16[512,256]{1,0:T(8,128)(2,1)} %refs_0_.10, bf16[512,256]{1,0:T(8,128)(2,1)} %copy-done.14, bf16[512,256]{1,0:T(8,128)(2,1)} %copy-done.6, bf16[512,256]{1,0:T(8,128)(2,1)} %copy-done.15, bf16[512,256]{1,0:T(8,128)(2,1)} %copy-done.7, ...), custom_call_target="tpu_custom_call" | custom-call | tf_op jit(solution)/shard_map/pallas_call | solution.py:199
  123.5 8.3 %shard_map.50.refs_16_ = f32[1024,512]{1,0:T(8,128)} custom-call(s32[2]{0:T(128)} %pad_add_fusion.me_ref.scalars, bf16[1024,2048]{1,0:T(8,128)(2,1)} %refs_7_.1, bf16[1024,2048]{1,0:T(8,128)(2,1)} %refs_7_.1, bf16[2,256,512]{2,1,0:T(8,128)(2,1)} %copy-done.11, bf16[2,256,512]{2,1,0:T(8,128)(2,1)} %copy-done.12, ...), custom_call_target="tpu_custom_call" | custom-call | tf_op jit(solution)/shard_map/pallas_call | solution.py:199
  131.9 0.8 copy-done.24
  132.7 0.2 copy-done.25
  132.9 11.7 %shard_map.52 = f32[1024,512]{1,0:T(8,128)} custom-call(s32[2]{0:T(128)} %pad_add_fusion.me_ref.scalars, bf16[1024,2048]{1,0:T(8,128)(2,1)} %refs_7_.1, bf16[1024,2048]{1,0:T(8,128)(2,1)} %refs_7_.1, bf16[1024,2048]{1,0:T(8,128)(2,1)} %refs_7_.1, bf16[1024,2048]{1,0:T(8,128)(2,1)} %refs_7_.1, bf16[1024,2048]{1,0:T(8,128)(2,1)} %refs_7_.1, ...), custom_call_target="tpu_custom_call" | custom-call | tf_op jit(solution)/shard_map/pallas_call | solution.py:199
  (64 shorter events, 0.2 us)
Async XLA Ops:
  0.0 9.7 %collective-permute-start.1 = (bf16[512,256]{1,0:T(8,128)(2,1)}, bf16[512,256]{1,0:T(8,128)(2,1)S(1)}, u32[]{:S(2)}, u32[]{:S(2)}) collective-permute-start(bf16[512,256]{1,0:T(8,128)(2,1)} %refs_0_.10), channel_id=1, source_target_pairs={{0,8},{4,12},{8,0},{12,4},{16,24},{20,28},{24,16},{28,20},{1,9},{5... | collective-permute-start | bytes 786440 | tf_op jit(solution)/shard_map/ppermute | solution.py:23
  3.0 8.0 %collective-permute-start.3 = (bf16[512,256]{1,0:T(8,128)(2,1)}, bf16[512,256]{1,0:T(8,128)(2,1)S(1)}, u32[]{:S(2)}, u32[]{:S(2)}) collective-permute-start(bf16[512,256]{1,0:T(8,128)(2,1)} %refs_0_.10), channel_id=1, source_target_pairs={{0,16},{4,20},{8,24},{12,28},{16,0},{20,4},{24,8},{28,12},{1,17},{... | collective-permute-start | bytes 786440 | tf_op jit(solution)/shard_map/ppermute | solution.py:23
  4.5 13.7 %collective-permute-start.7 = (bf16[512,256]{1,0:T(8,128)(2,1)}, bf16[512,256]{1,0:T(8,128)(2,1)S(1)}, u32[]{:S(2)}, u32[]{:S(2)}) collective-permute-start(bf16[512,256]{1,0:T(8,128)(2,1)} %refs_0_.10), channel_id=1, source_target_pairs={{0,1},{4,5},{8,9},{12,13},{16,17},{20,21},{24,25},{28,29}} | collective-permute-start | bytes 786440 | tf_op jit(solution)/shard_map/ppermute | solution.py:50
  8.0 12.6 %collective-permute-start.8 = (bf16[512,256]{1,0:T(8,128)(2,1)}, bf16[512,256]{1,0:T(8,128)(2,1)S(1)}, u32[]{:S(2)}, u32[]{:S(2)}) collective-permute-start(bf16[512,256]{1,0:T(8,128)(2,1)} %refs_0_.10), channel_id=1, source_target_pairs={{0,2},{4,6},{8,10},{12,14},{16,18},{20,22},{24,26},{28,30}} | collective-permute-start | bytes 786440 | tf_op jit(solution)/shard_map/ppermute | solution.py:50
  9.7 30.1 %copy-start.6 = (bf16[512,256]{1,0:T(8,128)(2,1)}, bf16[512,256]{1,0:T(8,128)(2,1)S(1)}, u32[]{:S(2)}) copy-start(bf16[512,256]{1,0:T(8,128)(2,1)S(1)} %collective-permute-done.1.refs_2_) | copy-start | bytes 786436
  10.9 28.8 %copy-start.7 = (bf16[512,256]{1,0:T(8,128)(2,1)}, bf16[512,256]{1,0:T(8,128)(2,1)S(1)}, u32[]{:S(2)}) copy-start(bf16[512,256]{1,0:T(8,128)(2,1)S(1)} %collective-permute-done.3.refs_4_) | copy-start | bytes 786436
  11.0 9.6 %collective-permute-start.5 = (bf16[512,256]{1,0:T(8,128)(2,1)S(1)}, bf16[512,256]{1,0:T(8,128)(2,1)S(1)}, u32[]{:S(2)}, u32[]{:S(2)}) collective-permute-start(bf16[512,256]{1,0:T(8,128)(2,1)S(1)} %broadcast_select_fusion.2), channel_id=1, source_target_pairs={{0,16},{4,12},{8,24},{12,4},{16,0},{20,28},{24,8},{28,20},{1,17},{... | collective-permute-start | bytes 786440 | tf_op jit(solution)/shard_map/ppermute | solution.py:33
  12.6 11.9 %collective-permute-start.9 = (bf16[512,256]{1,0:T(8,128)(2,1)}, bf16[512,256]{1,0:T(8,128)(2,1)S(1)}, u32[]{:S(2)}, u32[]{:S(2)}) collective-permute-start(bf16[512,256]{1,0:T(8,128)(2,1)} %refs_0_.10), channel_id=1, source_target_pairs={{0,3},{4,7},{8,11},{12,15},{16,19},{20,23},{24,27},{28,31}} | collective-permute-start | bytes 786440 | tf_op jit(solution)/shard_map/ppermute | solution.py:50
  18.1 7.4 %collective-permute-start = (bf16[512,256]{1,0:T(8,128)(2,1)}, bf16[512,256]{1,0:T(8,128)(2,1)S(1)}, u32[]{:S(2)}, u32[]{:S(2)}) collective-permute-start(bf16[512,256]{1,0:T(8,128)(2,1)} %refs_0_.10), channel_id=1, source_target_pairs={{0,4},{4,0},{8,12},{12,8},{16,20},{20,16},{24,28},{28,24},{1,5},{5... | collective-permute-start | bytes 786440 | tf_op jit(solution)/shard_map/ppermute | solution.py:23
  18.2 7.4 %collective-permute-start.2 = (bf16[512,256]{1,0:T(8,128)(2,1)S(1)}, bf16[512,256]{1,0:T(8,128)(2,1)S(1)}, u32[]{:S(2)}, u32[]{:S(2)}) collective-permute-start(bf16[512,256]{1,0:T(8,128)(2,1)S(1)} %collective-permute-done.1.refs_2_), channel_id=1, source_target_pairs={{0,4},{4,0},{8,12},{12,8},{16,20},{20,16},{24,28},{28,24},{1,5},{5... | collective-permute-start | bytes 786440 | tf_op jit(solution)/shard_map/ppermute | solution.py:23
  20.6 5.0 %collective-permute-start.4 = (bf16[512,256]{1,0:T(8,128)(2,1)S(1)}, bf16[512,256]{1,0:T(8,128)(2,1)S(1)}, u32[]{:S(2)}, u32[]{:S(2)}) collective-permute-start(bf16[512,256]{1,0:T(8,128)(2,1)S(1)} %collective-permute-done.3.refs_4_), channel_id=1, source_target_pairs={{0,4},{4,0},{8,12},{12,8},{16,20},{20,16},{24,28},{28,24},{1,5},{5... | collective-permute-start | bytes 786440 | tf_op jit(solution)/shard_map/ppermute | solution.py:23
  20.6 19.2 %copy-start.13 = (bf16[512,256]{1,0:T(8,128)(2,1)}, bf16[512,256]{1,0:T(8,128)(2,1)S(1)}, u32[]{:S(2)}) copy-start(bf16[512,256]{1,0:T(8,128)(2,1)S(1)} %collective-permute-done.5.refs_6_) | copy-start | bytes 786436
  20.6 5.0 %collective-permute-start.6 = (bf16[512,256]{1,0:T(8,128)(2,1)S(1)}, bf16[512,256]{1,0:T(8,128)(2,1)S(1)}, u32[]{:S(2)}, u32[]{:S(2)}) collective-permute-start(bf16[512,256]{1,0:T(8,128)(2,1)S(1)} %collective-permute-done.5.refs_6_), channel_id=1, source_target_pairs={{0,4},{4,0},{8,12},{12,8},{16,20},{20,16},{24,28},{28,24},{1,5},{5... | collective-permute-start | bytes 786440 | tf_op jit(solution)/shard_map/ppermute | solution.py:23
  25.5 18.6 %copy-start.5 = (bf16[512,256]{1,0:T(8,128)(2,1)}, bf16[512,256]{1,0:T(8,128)(2,1)S(1)}, u32[]{:S(2)}) copy-start(bf16[512,256]{1,0:T(8,128)(2,1)S(1)} %add_add_fusion.refs_0_) | copy-start | bytes 786436
  25.5 14.3 %copy-start.14 = (bf16[512,256]{1,0:T(8,128)(2,1)}, bf16[512,256]{1,0:T(8,128)(2,1)S(1)}, u32[]{:S(2)}) copy-start(bf16[512,256]{1,0:T(8,128)(2,1)S(1)} %collective-permute-done.refs_1_) | copy-start | bytes 786436
  25.5 14.2 %copy-start.15 = (bf16[512,256]{1,0:T(8,128)(2,1)}, bf16[512,256]{1,0:T(8,128)(2,1)S(1)}, u32[]{:S(2)}) copy-start(bf16[512,256]{1,0:T(8,128)(2,1)S(1)} %collective-permute-done.2.refs_3_) | copy-start | bytes 786436
  25.6 14.2 %copy-start.16 = (bf16[512,256]{1,0:T(8,128)(2,1)}, bf16[512,256]{1,0:T(8,128)(2,1)S(1)}, u32[]{:S(2)}) copy-start(bf16[512,256]{1,0:T(8,128)(2,1)S(1)} %collective-permute-done.4.refs_5_) | copy-start | bytes 786436
  25.6 14.2 %copy-start.17 = (bf16[512,256]{1,0:T(8,128)(2,1)}, bf16[512,256]{1,0:T(8,128)(2,1)S(1)}, u32[]{:S(2)}) copy-start(bf16[512,256]{1,0:T(8,128)(2,1)S(1)} %collective-permute-done.6.refs_7_) | copy-start | bytes 786436
  25.6 6.7 %collective-permute-start.11 = (bf16[512,256]{1,0:T(8,128)(2,1)S(1)}, bf16[512,256]{1,0:T(8,128)(2,1)S(1)}, u32[]{:S(2)}, u32[]{:S(2)}) collective-permute-start(bf16[512,256]{1,0:T(8,128)(2,1)S(1)} %add_add_fusion.refs_0_), channel_id=1, source_target_pairs={{0,8},{4,12},{8,0},{12,4},{16,24},{20,28},{24,16},{28,20},{1,9},{5... | collective-permute-start | bytes 786440 | tf_op jit(solution)/shard_map/ppermute | solution.py:23
  26.2 6.4 %collective-permute-start.13 = (bf16[512,256]{1,0:T(8,128)(2,1)S(1)}, bf16[512,256]{1,0:T(8,128)(2,1)S(1)}, u32[]{:S(2)}, u32[]{:S(2)}) collective-permute-start(bf16[512,256]{1,0:T(8,128)(2,1)S(1)} %add_add_fusion.refs_0_), channel_id=1, source_target_pairs={{0,16},{4,20},{8,24},{12,28},{16,0},{20,4},{24,8},{28,12},{1,17},{... | collective-permute-start | bytes 786440 | tf_op jit(solution)/shard_map/ppermute | solution.py:23
  32.3 11.8 %copy-start.8 = (bf16[512,256]{1,0:T(8,128)(2,1)}, bf16[512,256]{1,0:T(8,128)(2,1)S(1)}, u32[]{:S(2)}) copy-start(bf16[512,256]{1,0:T(8,128)(2,1)S(1)} %collective-permute-done.11.refs_2_) | copy-start | bytes 786436
  32.6 11.6 %copy-start.9 = (bf16[512,256]{1,0:T(8,128)(2,1)}, bf16[512,256]{1,0:T(8,128)(2,1)S(1)}, u32[]{:S(2)}) copy-start(bf16[512,256]{1,0:T(8,128)(2,1)S(1)} %collective-permute-done.13.refs_4_) | copy-start | bytes 786436
  32.6 6.5 %collective-permute-start.15 = (bf16[512,256]{1,0:T(8,128)(2,1)S(1)}, bf16[512,256]{1,0:T(8,128)(2,1)}, u32[]{:S(2)}, u32[]{:S(2)}) collective-permute-start(bf16[512,256]{1,0:T(8,128)(2,1)S(1)} %broadcast_select_fusion.1), channel_id=1, source_target_pairs={{0,16},{4,12},{8,24},{12,4},{16,0},{20,28},{24,8},{28,20},{1,17},{... | collective-permute-start | bytes 786440 | tf_op jit(solution)/shard_map/ppermute | solution.py:33
  33.9 10.2 %collective-permute-start.10 = (bf16[512,256]{1,0:T(8,128)(2,1)S(1)}, bf16[512,256]{1,0:T(8,128)(2,1)S(1)}, u32[]{:S(2)}, u32[]{:S(2)}) collective-permute-start(bf16[512,256]{1,0:T(8,128)(2,1)S(1)} %add_add_fusion.refs_0_), channel_id=1, source_target_pairs={{0,4},{4,0},{8,12},{12,8},{16,20},{20,16},{24,28},{28,24},{1,5},{5... | collective-permute-start | bytes 786440 | tf_op jit(solution)/shard_map/ppermute | solution.py:23
  33.9 10.2 %collective-permute-start.12 = (bf16[512,256]{1,0:T(8,128)(2,1)S(1)}, bf16[512,256]{1,0:T(8,128)(2,1)S(1)}, u32[]{:S(2)}, u32[]{:S(2)}) collective-permute-start(bf16[512,256]{1,0:T(8,128)(2,1)S(1)} %collective-permute-done.11.refs_2_), channel_id=1, source_target_pairs={{0,4},{4,0},{8,12},{12,8},{16,20},{20,16},{24,28},{28,24},{1,5},{5... | collective-permute-start | bytes 786440 | tf_op jit(solution)/shard_map/ppermute | solution.py:23
  34.4 9.7 %collective-permute-start.14 = (bf16[512,256]{1,0:T(8,128)(2,1)S(1)}, bf16[512,256]{1,0:T(8,128)(2,1)S(1)}, u32[]{:S(2)}, u32[]{:S(2)}) collective-permute-start(bf16[512,256]{1,0:T(8,128)(2,1)S(1)} %collective-permute-done.13.refs_4_), channel_id=1, source_target_pairs={{0,4},{4,0},{8,12},{12,8},{16,20},{20,16},{24,28},{28,24},{1,5},{5... | collective-permute-start | bytes 786440 | tf_op jit(solution)/shard_map/ppermute | solution.py:23
  39.2 4.9 %collective-permute-start.16 = (bf16[512,256]{1,0:T(8,128)(2,1)}, bf16[512,256]{1,0:T(8,128)(2,1)}, u32[]{:S(2)}, u32[]{:S(2)}) collective-permute-start(bf16[512,256]{1,0:T(8,128)(2,1)} %collective-permute-done.15.refs_6_.refs_0_), channel_id=1, source_target_pairs={{0,4},{4,0},{8,12},{12,8},{16,20},{20,16},{24,28},{28,24},{1,5},{5... | collective-permute-start | bytes 786440 | tf_op jit(solution)/shard_map/ppermute | solution.py:23
  44.1 0.7 copy-start.18
  44.1 0.8 copy-start.19
  44.1 0.9 copy-start.20
  49.3 2.5 %collective-permute-start.18 = (bf16[2,256,512]{2,1,0:T(8,128)(2,1)}, bf16[2,256,512]{2,1,0:T(8,128)(2,1)S(1)}, u32[]{:S(2)}, u32[]{:S(2)}) collective-permute-start(bf16[2,256,512]{2,1,0:T(8,128)(2,1)} %products.3.refs_2_.refs_6_.refs_8_), channel_id=1, source_target_pairs={{0,4},{4,0},{8,12},{12,8},{16,20},{20,16},{24,28},{28,24},{1,5},{5... | collective-permute-start | bytes 1572872 | tf_op jit(solution)/shard_map/ppermute | solution.py:23
  49.8 14.0 %collective-permute-start.19 = (bf16[2,256,512]{2,1,0:T(8,128)(2,1)}, bf16[2,256,512]{2,1,0:T(8,128)(2,1)S(1)}, u32[]{:S(2)}, u32[]{:S(2)}) collective-permute-start(bf16[2,256,512]{2,1,0:T(8,128)(2,1)} %products.3.refs_2_.refs_6_.refs_8_), channel_id=1, source_target_pairs={{0,16},{4,20},{8,24},{12,28},{16,0},{20,4},{24,8},{28,12},{1,17},{... | collective-permute-start | bytes 1572872 | tf_op jit(solution)/shard_map/ppermute | solution.py:23
  50.9 13.8 %collective-permute-start.17 = (bf16[2,256,512]{2,1,0:T(8,128)(2,1)}, bf16[2,256,512]{2,1,0:T(8,128)(2,1)S(1)}, u32[]{:S(2)}, u32[]{:S(2)}) collective-permute-start(bf16[2,256,512]{2,1,0:T(8,128)(2,1)} %products.3.refs_2_.refs_6_.refs_8_), channel_id=1, source_target_pairs={{0,8},{4,12},{8,0},{12,4},{16,24},{20,28},{24,16},{28,20},{1,9},{5... | collective-permute-start | bytes 1572872 | tf_op jit(solution)/shard_map/ppermute | solution.py:23
  51.8 0.8 copy-start.4
  63.8 2.8 %copy-start = (bf16[2,256,512]{2,1,0:T(8,128)(2,1)}, bf16[2,256,512]{2,1,0:T(8,128)(2,1)S(1)}, u32[]{:S(2)}) copy-start(bf16[2,256,512]{2,1,0:T(8,128)(2,1)S(1)} %collective-permute-done.19.refs_10_.refs_6_.refs_12_) | copy-start | bytes 1572868
  63.8 1.9 %collective-permute-start.22 = (bf16[2,256,512]{2,1,0:T(8,128)(2,1)S(1)}, bf16[2,256,512]{2,1,0:T(8,128)(2,1)S(1)}, u32[]{:S(2)}, u32[]{:S(2)}) collective-permute-start(bf16[2,256,512]{2,1,0:T(8,128)(2,1)S(1)} %collective-permute-done.19.refs_10_.refs_6_.refs_12_), channel_id=1, source_target_pairs={{0,4},{4,0},{8,12},{12,8},{16,20},{20,16},{24,28},{28,24},{1,5},{5... | collective-permute-start | bytes 1572872 | tf_op jit(solution)/shard_map/ppermute | solution.py:23
  64.7 1.9 %copy-start.1 = (bf16[2,256,512]{2,1,0:T(8,128)(2,1)}, bf16[2,256,512]{2,1,0:T(8,128)(2,1)S(1)}, u32[]{:S(2)}) copy-start(bf16[2,256,512]{2,1,0:T(8,128)(2,1)S(1)} %collective-permute-done.17.refs_8_.refs_4_.refs_10_) | copy-start | bytes 1572868
  64.7 1.9 %collective-permute-start.21 = (bf16[2,256,512]{2,1,0:T(8,128)(2,1)S(1)}, bf16[2,256,512]{2,1,0:T(8,128)(2,1)S(1)}, u32[]{:S(2)}, u32[]{:S(2)}) collective-permute-start(bf16[2,256,512]{2,1,0:T(8,128)(2,1)S(1)} %collective-permute-done.17.refs_8_.refs_4_.refs_10_), channel_id=1, source_target_pairs={{0,4},{4,0},{8,12},{12,8},{16,20},{20,16},{24,28},{28,24},{1,5},{5... | collective-permute-start | bytes 1572872 | tf_op jit(solution)/shard_map/ppermute | solution.py:23
  64.8 17.0 %collective-permute-start.20 = (bf16[2,256,512]{2,1,0:T(8,128)(2,1)S(1)}, bf16[2,256,512]{2,1,0:T(8,128)(2,1)S(1)}, u32[]{:S(2)}, u32[]{:S(2)}) collective-permute-start(bf16[2,256,512]{2,1,0:T(8,128)(2,1)S(1)} %broadcast_select_fusion), channel_id=1, source_target_pairs={{0,16},{4,12},{8,24},{12,4},{16,0},{20,28},{24,8},{28,20},{1,17},{... | collective-permute-start | bytes 1572872 | tf_op jit(solution)/shard_map/ppermute | solution.py:33
  65.7 0.9 copy-start.2
  66.6 0.8 copy-start.3
  75.7 6.3 %copy-start.10 = (bf16[2,256,512]{2,1,0:T(8,128)(2,1)S(1)}, bf16[2,256,512]{2,1,0:T(8,128)(2,1)}, u32[]{:S(2)}) copy-start(bf16[2,256,512]{2,1,0:T(8,128)(2,1)} %products.2.refs_8_) | copy-start | bytes 1572868
  81.8 3.7 %copy-start.11 = (bf16[2,256,512]{2,1,0:T(8,128)(2,1)}, bf16[2,256,512]{2,1,0:T(8,128)(2,1)S(1)}, u32[]{:S(2)}) copy-start(bf16[2,256,512]{2,1,0:T(8,128)(2,1)S(1)} %collective-permute-done.20.refs_2_.refs_14_) | copy-start | bytes 1572868
  81.8 3.7 %collective-permute-start.25 = (bf16[2,256,512]{2,1,0:T(8,128)(2,1)S(1)}, bf16[2,256,512]{2,1,0:T(8,128)(2,1)S(1)}, u32[]{:S(2)}, u32[]{:S(2)}) collective-permute-start(bf16[2,256,512]{2,1,0:T(8,128)(2,1)S(1)} %collective-permute-done.20.refs_2_.refs_14_), channel_id=1, source_target_pairs={{0,4},{4,0},{8,12},{12,8},{16,20},{20,16},{24,28},{28,24},{1,5},{5... | collective-permute-start | bytes 1572872 | tf_op jit(solution)/shard_map/ppermute | solution.py:23
  82.0 32.1 %collective-permute-start.29 = (bf16[2,256,512]{2,1,0:T(8,128)(2,1)S(1)}, bf16[2,256,512]{2,1,0:T(8,128)(2,1)S(1)}, u32[]{:S(2)}, u32[]{:S(2)}) collective-permute-start(bf16[2,256,512]{2,1,0:T(8,128)(2,1)S(1)} %copy-done.10), channel_id=1, source_target_pairs={{0,24},{4,28},{8,16},{12,20},{16,8},{20,12},{24,0},{28,4},{1,25},{... | collective-permute-start | bytes 1572872 | tf_op jit(solution)/shard_map/ppermute | solution.py:23
  83.8 30.9 %collective-permute-start.27 = (bf16[2,256,512]{2,1,0:T(8,128)(2,1)S(1)}, bf16[2,256,512]{2,1,0:T(8,128)(2,1)S(1)}, u32[]{:S(2)}, u32[]{:S(2)}) collective-permute-start(bf16[2,256,512]{2,1,0:T(8,128)(2,1)S(1)} %copy-done.10), channel_id=1, source_target_pairs={{0,16},{4,20},{8,24},{12,28},{16,0},{20,4},{24,8},{28,12},{1,17},{... | collective-permute-start | bytes 1572872 | tf_op jit(solution)/shard_map/ppermute | solution.py:23
  84.8 29.9 %collective-permute-start.24 = (bf16[2,256,512]{2,1,0:T(8,128)(2,1)S(1)}, bf16[2,256,512]{2,1,0:T(8,128)(2,1)S(1)}, u32[]{:S(2)}, u32[]{:S(2)}) collective-permute-start(bf16[2,256,512]{2,1,0:T(8,128)(2,1)S(1)} %copy-done.10), channel_id=1, source_target_pairs={{0,8},{4,12},{8,0},{12,4},{16,24},{20,28},{24,16},{28,20},{1,9},{5... | collective-permute-start | bytes 1572872 | tf_op jit(solution)/shard_map/ppermute | solution.py:23
  85.5 46.4 %collective-permute-start.23 = (bf16[2,256,512]{2,1,0:T(8,128)(2,1)S(1)}, bf16[2,256,512]{2,1,0:T(8,128)(2,1)}, u32[]{:S(2)}, u32[]{:S(2)}) collective-permute-start(bf16[2,256,512]{2,1,0:T(8,128)(2,1)S(1)} %copy-done.10), channel_id=1, source_target_pairs={{0,4},{4,0},{8,12},{12,8},{16,20},{20,16},{24,28},{28,24},{1,5},{5... | collective-permute-start | bytes 1572872 | tf_op jit(solution)/shard_map/ppermute | solution.py:23
  85.5 0.8 copy-start.12
  114.1 9.4 %copy-start.21 = (bf16[2,256,512]{2,1,0:T(8,128)(2,1)}, bf16[2,256,512]{2,1,0:T(8,128)(2,1)S(1)}, u32[]{:S(2)}) copy-start(bf16[2,256,512]{2,1,0:T(8,128)(2,1)S(1)} %collective-permute-done.29.refs_14_) | copy-start | bytes 1572868
  114.1 17.7 %collective-permute-start.30 = (bf16[2,256,512]{2,1,0:T(8,128)(2,1)S(1)}, bf16[2,256,512]{2,1,0:T(8,128)(2,1)S(1)}, u32[]{:S(2)}, u32[]{:S(2)}) collective-permute-start(bf16[2,256,512]{2,1,0:T(8,128)(2,1)S(1)} %collective-permute-done.29.refs_14_), channel_id=1, source_target_pairs={{0,4},{4,0},{8,12},{12,8},{16,20},{20,16},{24,28},{28,24},{1,5},{5... | collective-permute-start | bytes 1572872 | tf_op jit(solution)/shard_map/ppermute | solution.py:23
  114.6 8.9 %copy-start.22 = (bf16[2,256,512]{2,1,0:T(8,128)(2,1)}, bf16[2,256,512]{2,1,0:T(8,128)(2,1)S(1)}, u32[]{:S(2)}) copy-start(bf16[2,256,512]{2,1,0:T(8,128)(2,1)S(1)} %collective-permute-done.27.refs_12_) | copy-start | bytes 1572868
  114.6 17.2 %collective-permute-start.28 = (bf16[2,256,512]{2,1,0:T(8,128)(2,1)S(1)}, bf16[2,256,512]{2,1,0:T(8,128)(2,1)S(1)}, u32[]{:S(2)}, u32[]{:S(2)}) collective-permute-start(bf16[2,256,512]{2,1,0:T(8,128)(2,1)S(1)} %collective-permute-done.27.refs_12_), channel_id=1, source_target_pairs={{0,4},{4,0},{8,12},{12,8},{16,20},{20,16},{24,28},{28,24},{1,5},{5... | collective-permute-start | bytes 1572872 | tf_op jit(solution)/shard_map/ppermute | solution.py:23
  114.7 8.8 %copy-start.23 = (bf16[2,256,512]{2,1,0:T(8,128)(2,1)}, bf16[2,256,512]{2,1,0:T(8,128)(2,1)S(1)}, u32[]{:S(2)}) copy-start(bf16[2,256,512]{2,1,0:T(8,128)(2,1)S(1)} %collective-permute-done.24.refs_10_) | copy-start | bytes 1572868
  114.7 17.1 %collective-permute-start.26 = (bf16[2,256,512]{2,1,0:T(8,128)(2,1)S(1)}, bf16[2,256,512]{2,1,0:T(8,128)(2,1)}, u32[]{:S(2)}, u32[]{:S(2)}) collective-permute-start(bf16[2,256,512]{2,1,0:T(8,128)(2,1)S(1)} %collective-permute-done.24.refs_10_), channel_id=1, source_target_pairs={{0,4},{4,0},{8,12},{12,8},{16,20},{20,16},{24,28},{28,24},{1,5},{5... | collective-permute-start | bytes 1572872 | tf_op jit(solution)/shard_map/ppermute | solution.py:23
  131.8 0.9 copy-start.24
  131.8 1.0 copy-start.25
where the time goes:
time: 145 us
  Pallas kernels  84.8 us (58%)
  starting transfers between devices  28.8 us (20%)
  waiting for transfers between devices  24.4 us (17%)
  local copies, waits for them, and re-layouts  4.35 us (3%)
  other arithmetic  1.73 us (1%)
    pallas_call x7, Pallas kernels, call(): pl.pallas_call(kernel, grid_spec=pltpu.PrefetchScalarGridSpec(num_scalar_...  76.4 us
    ppermute x25, starting transfers between devices, swap(): return lax.ppermute(value, 'wide', [(i, i ^ mask) for i in range(count)])  14.4 us
    ppermute x25, waiting for transfers between devices, swap(): return lax.ppermute(value, 'wide', [(i, i ^ mask) for i in range(count)])  14.3 us
    ppermute x3, starting transfers between devices, from_first(): total = total + lax.ppermute(value, 'narrow', [(0, target)])  10.7 us
    pallas_call x2, Pallas kernels, products(): pl.pallas_call(products_kernel, out_shape=jax.ShapeDtypeStruct((2, size,...  8.47 us
    ppermute x3, waiting for transfers between devices, from_first(): total = total + lax.ppermute(value, 'narrow', [(0, target)])  5.32 us
    ppermute x3, waiting for transfers between devices, forward(): lax.ppermute(held, 'wide', [(i, i ^ (low if i % 2 else high)) for i in ra...  4.79 us
    unnamed x52, local copies, waits for them, and re-layouts  4.35 us
  transfers between devices with their start and end apart: 31, of which 9 were waited for; matrix products, arithmetic and copies ran while one was open for 1% of the time, Pallas kernels for 48%

commit v1 on v0

--- a/solution.py
+++ b/solution.py
@@ -395,19 +395,21 @@
         if bin(mask).count("1") > 1 and not begun:
             begun = True
             start = accumulate(scalars, height, tile, rows((0, 1)), firsts[:2])
+            total = accumulate(
+                scalars, order, tile, piece_lines(panels, tile, (0, 1)), firsts[:2]
+            )
             for bit in masks:
                 if bin(bit).count("1") == 1:
-                    firsts[bit] = after(firsts[bit], start)
+                    firsts[bit] = after(firsts[bit], start, total)
                     firsts[bit + 1] = swap(firsts[bit], 1, count)
         firsts[mask] = forward(firsts, mask, count)
     for mask in masks:
         if firsts[mask + 1] is None and mask != count - 2:
             firsts[mask + 1] = swap(firsts[mask], 1, count)
     total = accumulate(
-        scalars, order, tile, piece_lines(panels, tile, range(count - 2)), firsts[:-2]
-    )
-    middle = accumulate(scalars, height, tile, rows(early), firsts[2:-2], start)
-    firsts[-2] = after(firsts[-2], total, middle)
+        scalars, order, tile, piece_lines(panels, tile, early), firsts[2:-2], total
+    )
+    firsts[-2] = after(firsts[-2], total)
     firsts[-1] = swap(firsts[-2], 1, count)
 
     owns = [own] + [None] * (count - 1)
@@ -423,7 +425,15 @@
         scalars, order, tile, piece_lines(columns, tile, every), firsts, inverse, scale, True
     )
     panel_cols = project(
-        scalars, height, tile, rows(late), firsts[-2:], inverse, scale, False, middle
+        scalars,
+        height,
+        2 * tile,
+        row_lines(row_vectors, scalars, share, 2 * tile, range(2, count)),
+        firsts[2:],
+        inverse,
+        scale,
+        False,
+        start,
     )
     return update(scalars, height, tile, rows(every), owns, panel_cols, solved, scale)
 

time: 145 us -> 141 us (0.972)
  waiting for transfers between devices: 24.4 us -> 21.4 us
  Pallas kernels: 84.8 us -> 82.1 us
    ppermute x25, waiting for transfers between devices: 14.3 us -> 9.6 us  [swap(): return lax.ppermute(value, 'wide', [(i, i ^ mask) for i in range(count)])]
    pallas_call x7, Pallas kernels: 76.4 us -> 73.6 us  [call(): pl.pallas_call(kernel, grid_spec=pltpu.PrefetchScalarGridSpec(num_scalar_...]
    ppermute x3, waiting for transfers between devices: 4.79 us -> 6.52 us  [forward(): lax.ppermute(held, 'wide', [(i, i ^ (low if i % 2 else high)) for i in ra...]
  transfers between devices with their start and end apart: 31 -> 31, of which waited for: 9 -> 10; matrix products, arithmetic and copies ran while one was open for 1% -> 2% of each run, Pallas kernels for 48% -> 47%
where the time goes in v1:
time: 141 us; the launch traced here: 140 us
  Pallas kernels  82.1 us (58%)
  starting transfers between devices  28.6 us (20%)
  waiting for transfers between devices  21.4 us (15%)
  local copies, waits for them, and re-layouts  4.97 us (4%)
  other arithmetic  2.62 us (2%)
    pallas_call x7, Pallas kernels, call(): pl.pallas_call(kernel, grid_spec=pltpu.PrefetchScalarGridSpec(num_scalar_...  73.6 us
    ppermute x25, starting transfers between devices, swap(): return lax.ppermute(value, 'wide', [(i, i ^ mask) for i in range(count)])  14.3 us
    ppermute x3, starting transfers between devices, from_first(): total = total + lax.ppermute(value, 'narrow', [(0, target)])  10.7 us
    ppermute x25, waiting for transfers between devices, swap(): return lax.ppermute(value, 'wide', [(i, i ^ mask) for i in range(count)])  9.6 us
    pallas_call x2, Pallas kernels, products(): pl.pallas_call(products_kernel, out_shape=jax.ShapeDtypeStruct((2, size,...  8.47 us
    ppermute x3, waiting for transfers between devices, forward(): lax.ppermute(held, 'wide', [(i, i ^ (low if i % 2 else high)) for i in ra...  6.52 us
    ppermute x3, waiting for transfers between devices, from_first(): total = total + lax.ppermute(value, 'narrow', [(0, target)])  5.32 us
    unnamed x52, local copies, waits for them, and re-layouts  4.97 us
  transfers between devices with their start and end apart: 31, of which 10 were waited for; matrix products, arithmetic and copies ran while one was open for 2% of the time, Pallas kernels for 47%

profile of v1, /device:TPU:0, one launch (start us, length us, event | category | flops | bytes accessed | tf_op | source)
XLA Modules:
  0.0 140.3 jit_solution(16505775948891481289)
XLA Ops:
  0.0 3.0 %collective-permute-start.1 = (bf16[512,256]{1,0:T(8,128)(2,1)}, bf16[512,256]{1,0:T(8,128)(2,1)S(1)}, u32[]{:S(2)}, u32[]{:S(2)}) collective-permute-start(bf16[512,256]{1,0:T(8,128)(2,1)} %refs_0_.8), channel_id=1, source_target_pairs={{0,8},{4,12},{8,0},{12,4},{16,24},{20,28},{24,16},{28,20},{1,9},{5... | collective-permute-start | bytes 786440 | tf_op jit(solution)/shard_map/ppermute | solution.py:23
  3.0 1.5 %collective-permute-start.3 = (bf16[512,256]{1,0:T(8,128)(2,1)}, bf16[512,256]{1,0:T(8,128)(2,1)S(1)}, u32[]{:S(2)}, u32[]{:S(2)}) collective-permute-start(bf16[512,256]{1,0:T(8,128)(2,1)} %refs_0_.8), channel_id=1, source_target_pairs={{0,16},{4,20},{8,24},{12,28},{16,0},{20,4},{24,8},{28,12},{1,17},{... | collective-permute-start | bytes 786440 | tf_op jit(solution)/shard_map/ppermute | solution.py:23
  4.5 3.5 %collective-permute-start.7 = (bf16[512,256]{1,0:T(8,128)(2,1)}, bf16[512,256]{1,0:T(8,128)(2,1)S(1)}, u32[]{:S(2)}, u32[]{:S(2)}) collective-permute-start(bf16[512,256]{1,0:T(8,128)(2,1)} %refs_0_.8), channel_id=1, source_target_pairs={{0,1},{4,5},{8,9},{12,13},{16,17},{20,21},{24,25},{28,29}} | collective-permute-start | bytes 786440 | tf_op jit(solution)/shard_map/ppermute | solution.py:50
  8.0 1.7 %collective-permute-start.8 = (bf16[512,256]{1,0:T(8,128)(2,1)}, bf16[512,256]{1,0:T(8,128)(2,1)S(1)}, u32[]{:S(2)}, u32[]{:S(2)}) collective-permute-start(bf16[512,256]{1,0:T(8,128)(2,1)} %refs_0_.8), channel_id=1, source_target_pairs={{0,2},{4,6},{8,10},{12,14},{16,18},{20,22},{24,26},{28,30}} | collective-permute-start | bytes 786440 | tf_op jit(solution)/shard_map/ppermute | solution.py:50
  9.7 1.2 collective-permute-done.3.refs_4_
  11.0 1.6 %collective-permute-start.5 = (bf16[512,256]{1,0:T(8,128)(2,1)S(1)}, bf16[512,256]{1,0:T(8,128)(2,1)S(1)}, u32[]{:S(2)}, u32[]{:S(2)}) collective-permute-start(bf16[512,256]{1,0:T(8,128)(2,1)S(1)} %broadcast_select_fusion.2), channel_id=1, source_target_pairs={{0,16},{4,12},{8,24},{12,4},{16,0},{20,28},{24,8},{28,20},{1,17},{... | collective-permute-start | bytes 786440 | tf_op jit(solution)/shard_map/ppermute | solution.py:33
  12.6 5.5 %collective-permute-start.9 = (bf16[512,256]{1,0:T(8,128)(2,1)}, bf16[512,256]{1,0:T(8,128)(2,1)S(1)}, u32[]{:S(2)}, u32[]{:S(2)}) collective-permute-start(bf16[512,256]{1,0:T(8,128)(2,1)} %refs_0_.8), channel_id=1, source_target_pairs={{0,3},{4,7},{8,11},{12,15},{16,19},{20,23},{24,27},{28,31}} | collective-permute-start | bytes 786440 | tf_op jit(solution)/shard_map/ppermute | solution.py:50
  18.1 0.1 collective-permute-start
  18.2 0.0 collective-permute-done.7
  18.2 0.5 collective-permute-start.2
  18.7 1.9 %collective-permute-done.8 = bf16[512,256]{1,0:T(8,128)(2,1)S(1)} collective-permute-done((bf16[512,256]{1,0:T(8,128)(2,1)}, bf16[512,256]{1,0:T(8,128)(2,1)S(1)}, u32[]{:S(2)}, u32[]{:S(2)}) %collective-permute-start.8) | collective-permute-done | bytes 262176 | tf_op jit(solution)/shard_map/ppermute | solution.py:50
  20.6 0.0 collective-permute-start.4
  20.6 0.0 collective-permute-done.5.refs_6_
  20.6 0.5 collective-permute-start.6
  21.1 3.4 %collective-permute-done.9 = bf16[512,256]{1,0:T(8,128)(2,1)S(1)} collective-permute-done((bf16[512,256]{1,0:T(8,128)(2,1)}, bf16[512,256]{1,0:T(8,128)(2,1)S(1)}, u32[]{:S(2)}, u32[]{:S(2)}) %collective-permute-start.9) | collective-permute-done | bytes 262176 | tf_op jit(solution)/shard_map/ppermute | solution.py:50
  24.5 1.0 add_add_fusion.refs_0_
  25.5 0.0 collective-permute-done.refs_1_
  25.6 0.0 collective-permute-done.4.refs_5_
  25.6 0.0 collective-permute-done.6.refs_7_
  25.6 0.6 collective-permute-start.11
  26.2 0.5 collective-permute-start.13
  26.7 5.6 %collective-permute-done.11.refs_2_.refs_0_ = bf16[512,256]{1,0:T(8,128)(2,1)S(1)} collective-permute-done((bf16[512,256]{1,0:T(8,128)(2,1)S(1)}, bf16[512,256]{1,0:T(8,128)(2,1)S(1)}, u32[]{:S(2)}, u32[]{:S(2)}) %collective-permute-start.11) | collective-permute-done | bytes 262176 | tf_op jit(solution)/shard_map/ppermute | solution.py:23
  32.3 0.3 collective-permute-done.13.refs_4_.refs_2_
  32.6 1.2 collective-permute-start.15
  33.9 0.5 collective-permute-start.12
  34.4 0.0 collective-permute-start.14
  34.4 4.8 %collective-permute-done.15.refs_6_.refs_0_ = bf16[512,256]{1,0:T(8,128)(2,1)} collective-permute-done((bf16[512,256]{1,0:T(8,128)(2,1)S(1)}, bf16[512,256]{1,0:T(8,128)(2,1)}, u32[]{:S(2)}, u32[]{:S(2)}) %collective-permute-start.15) | collective-permute-done | bytes 262176 | tf_op jit(solution)/shard_map/ppermute | solution.py:33
  39.2 0.0 collective-permute-start.16
  39.2 0.6 pad_add_fusion.me_ref.scalars
  39.8 4.2 %products.2.refs_8_ = bf16[2,256,512]{2,1,0:T(8,128)(2,1)} custom-call(s32[2]{0:T(128)} %pad_add_fusion.me_ref.scalars, bf16[256,2048]{1,0:T(8,128)(2,1)} %primal_ref.3, bf16[256,2048]{1,0:T(8,128)(2,1)} %dual_ref.3, bf16[512,256]{1,0:T(8,128)(2,1)} %refs_0_.8, bf16[512,256]{1,0:T(8,128)(2,1)} %copy-done.14, bf16[512,256]{1,0:T(8,128)(2,1)} %copy-done.5, ...), custom_call_target="tpu_custom_call" | custom-call | tf_op jit(solution)/shard_map/products/pallas_call | solution.py:158
  44.1 0.0 collective-permute-done.10.refs_1_
  44.1 0.0 collective-permute-done.16.refs_7_.refs_1_
  44.1 0.7 copy-done.18
  44.8 0.1 copy-done.19
  44.9 0.1 copy-done.20
  45.0 4.2 %products.3.refs_2_.refs_8_ = bf16[2,256,512]{2,1,0:T(8,128)(2,1)} custom-call(s32[2]{0:T(128)} %pad_add_fusion.me_ref.scalars, bf16[256,2048]{1,0:T(8,128)(2,1)} %primal_ref.3, bf16[256,2048]{1,0:T(8,128)(2,1)} %dual_ref.3, bf16[512,256]{1,0:T(8,128)(2,1)} %copy-done.7, bf16[512,256]{1,0:T(8,128)(2,1)} %copy-done.18, bf16[512,256]{1,0:T(8,128)(2,1)} %copy-done.8, ...), custom_call_target="tpu_custom_call" | custom-call | tf_op jit(solution)/shard_map/products/pallas_call | solution.py:158
  49.2 0.5 collective-permute-start.18
  49.7 1.2 collective-permute-start.19
  50.9 0.8 collective-permute-start.17
  51.8 0.8 copy-done.4
  52.6 3.9 %shard_map.47.refs_8_ = f32[2,512,512]{2,1,0:T(8,128)} custom-call(s32[2]{0:T(128)} %pad_add_fusion.me_ref.scalars, bf16[512,256]{1,0:T(8,128)(2,1)} %copy-done.7, bf16[512,256]{1,0:T(8,128)(2,1)} %copy-done.18, bf16[2,256,512]{2,1,0:T(8,128)(2,1)} %products.3.refs_2_.refs_8_, bf16[2,256,512]{2,1,0:T(8,128)(2,1)} %copy-done.4), custom_call_target="tpu_custom_call" | custom-call | tf_op jit(solution)/shard_map/pallas_call | solution.py:199
  56.5 5.9 %shard_map.46.refs_13_ = f32[2,1024,512]{2,1,0:T(8,128)} custom-call(s32[2]{0:T(128)} %pad_add_fusion.me_ref.scalars, bf16[1024,2048]{1,0:T(8,128)(2,1)} %refs_7_.1, bf16[1024,2048]{1,0:T(8,128)(2,1)} %refs_7_.1, bf16[2,256,512]{2,1,0:T(8,128)(2,1)} %products.3.refs_2_.refs_8_, bf16[2,256,512]{2,1,0:T(8,128)(2,1)} %copy-done.4), custom_call_target="tpu_custom_call" | custom-call | tf_op jit(solution)/shard_map/pallas_call | solution.py:199
  62.3 1.5 %collective-permute-done.19.refs_6_.refs_8_.refs_12_ = bf16[2,256,512]{2,1,0:T(8,128)(2,1)S(1)} collective-permute-done((bf16[2,256,512]{2,1,0:T(8,128)(2,1)}, bf16[2,256,512]{2,1,0:T(8,128)(2,1)S(1)}, u32[]{:S(2)}, u32[]{:S(2)}) %collective-permute-start.19) | collective-permute-done | bytes 524320 | tf_op jit(solution)/shard_map/ppermute | solution.py:23
  63.8 0.9 collective-permute-done.17.refs_4_.refs_6_.refs_10_
  64.7 0.9 broadcast_select_fusion
  65.6 0.8 collective-permute-start.20
  66.5 0.1 collective-permute-done.21.refs_5_.refs_7_.refs_11_
  66.6 0.7 copy-done.2
  67.3 0.8 copy-done.3
  68.1 5.2 %shard_map.48.refs_4_ = f32[2,512,512]{2,1,0:T(8,128)} custom-call(s32[2]{0:T(128)} %pad_add_fusion.me_ref.scalars, bf16[512,256]{1,0:T(8,128)(2,1)} %copy-done.8, bf16[512,256]{1,0:T(8,128)(2,1)} %copy-done.19, bf16[512,256]{1,0:T(8,128)(2,1)} %copy-done.9, bf16[512,256]{1,0:T(8,128)(2,1)} %copy-done.20, ...), custom_call_target="tpu_custom_call", output_to_operand_aliasing={{}: (9, {})} | custom-call | tf_op jit(solution)/shard_map/pallas_call | solution.py:199
  73.3 1.7 %collective-permute-done.20.refs_2_.refs_10_.refs_14_ = bf16[2,256,512]{2,1,0:T(8,128)(2,1)S(1)} collective-permute-done((bf16[2,256,512]{2,1,0:T(8,128)(2,1)}, bf16[2,256,512]{2,1,0:T(8,128)(2,1)S(1)}, u32[]{:S(2)}, u32[]{:S(2)}) %collective-permute-start.20) | collective-permute-done | bytes 524320 | tf_op jit(solution)/shard_map/ppermute | solution.py:33
  75.0 1.8 %collective-permute-start.29 = (bf16[2,256,512]{2,1,0:T(8,128)(2,1)S(1)}, bf16[2,256,512]{2,1,0:T(8,128)(2,1)S(1)}, u32[]{:S(2)}, u32[]{:S(2)}) collective-permute-start(bf16[2,256,512]{2,1,0:T(8,128)(2,1)S(1)} %copy-done.10), channel_id=1, source_target_pairs={{0,24},{4,28},{8,16},{12,20},{16,8},{20,12},{24,0},{28,4},{1,25},{... | collective-permute-start | bytes 1572872 | tf_op jit(solution)/shard_map/ppermute | solution.py:23
  76.9 0.7 collective-permute-start.27
  77.6 1.0 collective-permute-start.24
  78.6 0.8 copy-done.12
  79.4 27.8 %shard_map.49.refs_12_.refs_16_ = bf16[2,512,512]{2,1,0:T(8,128)(2,1)} custom-call(s32[2]{0:T(128)} %pad_add_fusion.me_ref.scalars, bf16[512,256]{1,0:T(8,128)(2,1)} %collective-permute-done.15.refs_6_.refs_0_, bf16[512,256]{1,0:T(8,128)(2,1)} %collective-permute-done.16.refs_7_.refs_1_, bf16[2,256,512]{2,1,0:T(8,128)(2,1)} %copy-done.11, ...), custom_call_target="tpu_custom_call" | custom-call | flops 15000000512 | bytes 2097152 | tf_op jit(solution)/shard_map/pallas_call | solution.py:199
  107.2 0.5 collective-permute-start.30
  107.7 0.1 collective-permute-start.28
  107.8 0.4 collective-permute-start.26
  108.3 8.3 %shard_map.51.refs_17_ = bf16[2,512,512]{2,1,0:T(8,128)(2,1)} custom-call(s32[2]{0:T(128)} %pad_add_fusion.me_ref.scalars, bf16[512,256]{1,0:T(8,128)(2,1)} %refs_0_.8, bf16[512,256]{1,0:T(8,128)(2,1)} %copy-done.14, bf16[512,256]{1,0:T(8,128)(2,1)} %copy-done.5, bf16[512,256]{1,0:T(8,128)(2,1)} %copy-done.15, bf16[512,256]{1,0:T(8,128)(2,1)} %copy-done.6, ...), custom_call_target="tpu_custom_call" | custom-call | tf_op jit(solution)/shard_map/pallas_call | solution.py:199
  116.6 10.7 %shard_map.50.refs_16_ = f32[1024,512]{1,0:T(8,128)} custom-call(s32[2]{0:T(128)} %pad_add_fusion.me_ref.scalars, bf16[1024,2048]{1,0:T(8,128)(2,1)} %refs_7_.1, bf16[1024,2048]{1,0:T(8,128)(2,1)} %refs_7_.1, bf16[1024,2048]{1,0:T(8,128)(2,1)} %refs_7_.1, bf16[1024,2048]{1,0:T(8,128)(2,1)} %refs_7_.1, bf16[1024,2048]{1,0:T(8,128)(2,1)} %refs_7_.1, ...), custom_call_target="tpu_custom_call" | custom-call | tf_op jit(solution)/shard_map/pallas_call | solution.py:199
  127.4 0.8 copy-done.24
  128.2 0.2 copy-done.25
  128.4 11.7 %shard_map.52 = f32[1024,512]{1,0:T(8,128)} custom-call(s32[2]{0:T(128)} %pad_add_fusion.me_ref.scalars, bf16[1024,2048]{1,0:T(8,128)(2,1)} %refs_7_.1, bf16[1024,2048]{1,0:T(8,128)(2,1)} %refs_7_.1, bf16[1024,2048]{1,0:T(8,128)(2,1)} %refs_7_.1, bf16[1024,2048]{1,0:T(8,128)(2,1)} %refs_7_.1, bf16[1024,2048]{1,0:T(8,128)(2,1)} %refs_7_.1, ...), custom_call_target="tpu_custom_call" | custom-call | tf_op jit(solution)/shard_map/pallas_call | solution.py:199
  (64 shorter events, 0.2 us)
Async XLA Ops:
  0.0 9.7 %collective-permute-start.1 = (bf16[512,256]{1,0:T(8,128)(2,1)}, bf16[512,256]{1,0:T(8,128)(2,1)S(1)}, u32[]{:S(2)}, u32[]{:S(2)}) collective-permute-start(bf16[512,256]{1,0:T(8,128)(2,1)} %refs_0_.8), channel_id=1, source_target_pairs={{0,8},{4,12},{8,0},{12,4},{16,24},{20,28},{24,16},{28,20},{1,9},{5... | collective-permute-start | bytes 786440 | tf_op jit(solution)/shard_map/ppermute | solution.py:23
  3.0 8.0 %collective-permute-start.3 = (bf16[512,256]{1,0:T(8,128)(2,1)}, bf16[512,256]{1,0:T(8,128)(2,1)S(1)}, u32[]{:S(2)}, u32[]{:S(2)}) collective-permute-start(bf16[512,256]{1,0:T(8,128)(2,1)} %refs_0_.8), channel_id=1, source_target_pairs={{0,16},{4,20},{8,24},{12,28},{16,0},{20,4},{24,8},{28,12},{1,17},{... | collective-permute-start | bytes 786440 | tf_op jit(solution)/shard_map/ppermute | solution.py:23
  4.5 13.7 %collective-permute-start.7 = (bf16[512,256]{1,0:T(8,128)(2,1)}, bf16[512,256]{1,0:T(8,128)(2,1)S(1)}, u32[]{:S(2)}, u32[]{:S(2)}) collective-permute-start(bf16[512,256]{1,0:T(8,128)(2,1)} %refs_0_.8), channel_id=1, source_target_pairs={{0,1},{4,5},{8,9},{12,13},{16,17},{20,21},{24,25},{28,29}} | collective-permute-start | bytes 786440 | tf_op jit(solution)/shard_map/ppermute | solution.py:50
  8.0 12.6 %collective-permute-start.8 = (bf16[512,256]{1,0:T(8,128)(2,1)}, bf16[512,256]{1,0:T(8,128)(2,1)S(1)}, u32[]{:S(2)}, u32[]{:S(2)}) collective-permute-start(bf16[512,256]{1,0:T(8,128)(2,1)} %refs_0_.8), channel_id=1, source_target_pairs={{0,2},{4,6},{8,10},{12,14},{16,18},{20,22},{24,26},{28,30}} | collective-permute-start | bytes 786440 | tf_op jit(solution)/shard_map/ppermute | solution.py:50
  9.7 30.1 %copy-start.5 = (bf16[512,256]{1,0:T(8,128)(2,1)}, bf16[512,256]{1,0:T(8,128)(2,1)S(1)}, u32[]{:S(2)}) copy-start(bf16[512,256]{1,0:T(8,128)(2,1)S(1)} %collective-permute-done.1.refs_2_) | copy-start | bytes 786436
  10.9 28.8 %copy-start.6 = (bf16[512,256]{1,0:T(8,128)(2,1)}, bf16[512,256]{1,0:T(8,128)(2,1)S(1)}, u32[]{:S(2)}) copy-start(bf16[512,256]{1,0:T(8,128)(2,1)S(1)} %collective-permute-done.3.refs_4_) | copy-start | bytes 786436
  11.0 9.6 %collective-permute-start.5 = (bf16[512,256]{1,0:T(8,128)(2,1)S(1)}, bf16[512,256]{1,0:T(8,128)(2,1)S(1)}, u32[]{:S(2)}, u32[]{:S(2)}) collective-permute-start(bf16[512,256]{1,0:T(8,128)(2,1)S(1)} %broadcast_select_fusion.2), channel_id=1, source_target_pairs={{0,16},{4,12},{8,24},{12,4},{16,0},{20,28},{24,8},{28,20},{1,17},{... | collective-permute-start | bytes 786440 | tf_op jit(solution)/shard_map/ppermute | solution.py:33
  12.6 11.9 %collective-permute-start.9 = (bf16[512,256]{1,0:T(8,128)(2,1)}, bf16[512,256]{1,0:T(8,128)(2,1)S(1)}, u32[]{:S(2)}, u32[]{:S(2)}) collective-permute-start(bf16[512,256]{1,0:T(8,128)(2,1)} %refs_0_.8), channel_id=1, source_target_pairs={{0,3},{4,7},{8,11},{12,15},{16,19},{20,23},{24,27},{28,31}} | collective-permute-start | bytes 786440 | tf_op jit(solution)/shard_map/ppermute | solution.py:50
  18.1 7.4 %collective-permute-start = (bf16[512,256]{1,0:T(8,128)(2,1)}, bf16[512,256]{1,0:T(8,128)(2,1)S(1)}, u32[]{:S(2)}, u32[]{:S(2)}) collective-permute-start(bf16[512,256]{1,0:T(8,128)(2,1)} %refs_0_.8), channel_id=1, source_target_pairs={{0,4},{4,0},{8,12},{12,8},{16,20},{20,16},{24,28},{28,24},{1,5},{5... | collective-permute-start | bytes 786440 | tf_op jit(solution)/shard_map/ppermute | solution.py:23
  18.2 7.4 %collective-permute-start.2 = (bf16[512,256]{1,0:T(8,128)(2,1)S(1)}, bf16[512,256]{1,0:T(8,128)(2,1)S(1)}, u32[]{:S(2)}, u32[]{:S(2)}) collective-permute-start(bf16[512,256]{1,0:T(8,128)(2,1)S(1)} %collective-permute-done.1.refs_2_), channel_id=1, source_target_pairs={{0,4},{4,0},{8,12},{12,8},{16,20},{20,16},{24,28},{28,24},{1,5},{5... | collective-permute-start | bytes 786440 | tf_op jit(solution)/shard_map/ppermute | solution.py:23
  20.6 5.0 %collective-permute-start.4 = (bf16[512,256]{1,0:T(8,128)(2,1)S(1)}, bf16[512,256]{1,0:T(8,128)(2,1)S(1)}, u32[]{:S(2)}, u32[]{:S(2)}) collective-permute-start(bf16[512,256]{1,0:T(8,128)(2,1)S(1)} %collective-permute-done.3.refs_4_), channel_id=1, source_target_pairs={{0,4},{4,0},{8,12},{12,8},{16,20},{20,16},{24,28},{28,24},{1,5},{5... | collective-permute-start | bytes 786440 | tf_op jit(solution)/shard_map/ppermute | solution.py:23
  20.6 19.2 %copy-start.13 = (bf16[512,256]{1,0:T(8,128)(2,1)}, bf16[512,256]{1,0:T(8,128)(2,1)S(1)}, u32[]{:S(2)}) copy-start(bf16[512,256]{1,0:T(8,128)(2,1)S(1)} %collective-permute-done.5.refs_6_) | copy-start | bytes 786436
  20.6 5.0 %collective-permute-start.6 = (bf16[512,256]{1,0:T(8,128)(2,1)S(1)}, bf16[512,256]{1,0:T(8,128)(2,1)S(1)}, u32[]{:S(2)}, u32[]{:S(2)}) collective-permute-start(bf16[512,256]{1,0:T(8,128)(2,1)S(1)} %collective-permute-done.5.refs_6_), channel_id=1, source_target_pairs={{0,4},{4,0},{8,12},{12,8},{16,20},{20,16},{24,28},{28,24},{1,5},{5... | collective-permute-start | bytes 786440 | tf_op jit(solution)/shard_map/ppermute | solution.py:23
  25.5 18.5 %copy-start.7 = (bf16[512,256]{1,0:T(8,128)(2,1)}, bf16[512,256]{1,0:T(8,128)(2,1)S(1)}, u32[]{:S(2)}) copy-start(bf16[512,256]{1,0:T(8,128)(2,1)S(1)} %add_add_fusion.refs_0_) | copy-start | bytes 786436
  25.5 14.3 %copy-start.14 = (bf16[512,256]{1,0:T(8,128)(2,1)}, bf16[512,256]{1,0:T(8,128)(2,1)S(1)}, u32[]{:S(2)}) copy-start(bf16[512,256]{1,0:T(8,128)(2,1)S(1)} %collective-permute-done.refs_1_) | copy-start | bytes 786436
  25.5 14.2 %copy-start.15 = (bf16[512,256]{1,0:T(8,128)(2,1)}, bf16[512,256]{1,0:T(8,128)(2,1)S(1)}, u32[]{:S(2)}) copy-start(bf16[512,256]{1,0:T(8,128)(2,1)S(1)} %collective-permute-done.2.refs_3_) | copy-start | bytes 786436
  25.6 14.2 %copy-start.16 = (bf16[512,256]{1,0:T(8,128)(2,1)}, bf16[512,256]{1,0:T(8,128)(2,1)S(1)}, u32[]{:S(2)}) copy-start(bf16[512,256]{1,0:T(8,128)(2,1)S(1)} %collective-permute-done.4.refs_5_) | copy-start | bytes 786436
  25.6 14.2 %copy-start.17 = (bf16[512,256]{1,0:T(8,128)(2,1)}, bf16[512,256]{1,0:T(8,128)(2,1)S(1)}, u32[]{:S(2)}) copy-start(bf16[512,256]{1,0:T(8,128)(2,1)S(1)} %collective-permute-done.6.refs_7_) | copy-start | bytes 786436
  25.6 6.7 %collective-permute-start.11 = (bf16[512,256]{1,0:T(8,128)(2,1)S(1)}, bf16[512,256]{1,0:T(8,128)(2,1)S(1)}, u32[]{:S(2)}, u32[]{:S(2)}) collective-permute-start(bf16[512,256]{1,0:T(8,128)(2,1)S(1)} %add_add_fusion.refs_0_), channel_id=1, source_target_pairs={{0,8},{4,12},{8,0},{12,4},{16,24},{20,28},{24,16},{28,20},{1,9},{5... | collective-permute-start | bytes 786440 | tf_op jit(solution)/shard_map/ppermute | solution.py:23
  26.2 6.4 %collective-permute-start.13 = (bf16[512,256]{1,0:T(8,128)(2,1)S(1)}, bf16[512,256]{1,0:T(8,128)(2,1)S(1)}, u32[]{:S(2)}, u32[]{:S(2)}) collective-permute-start(bf16[512,256]{1,0:T(8,128)(2,1)S(1)} %add_add_fusion.refs_0_), channel_id=1, source_target_pairs={{0,16},{4,20},{8,24},{12,28},{16,0},{20,4},{24,8},{28,12},{1,17},{... | collective-permute-start | bytes 786440 | tf_op jit(solution)/shard_map/ppermute | solution.py:23
  32.3 11.8 %copy-start.8 = (bf16[512,256]{1,0:T(8,128)(2,1)}, bf16[512,256]{1,0:T(8,128)(2,1)S(1)}, u32[]{:S(2)}) copy-start(bf16[512,256]{1,0:T(8,128)(2,1)S(1)} %collective-permute-done.11.refs_2_.refs_0_) | copy-start | bytes 786436
  32.6 11.5 %copy-start.9 = (bf16[512,256]{1,0:T(8,128)(2,1)}, bf16[512,256]{1,0:T(8,128)(2,1)S(1)}, u32[]{:S(2)}) copy-start(bf16[512,256]{1,0:T(8,128)(2,1)S(1)} %collective-permute-done.13.refs_4_.refs_2_) | copy-start | bytes 786436
  32.6 6.5 %collective-permute-start.15 = (bf16[512,256]{1,0:T(8,128)(2,1)S(1)}, bf16[512,256]{1,0:T(8,128)(2,1)}, u32[]{:S(2)}, u32[]{:S(2)}) collective-permute-start(bf16[512,256]{1,0:T(8,128)(2,1)S(1)} %broadcast_select_fusion.1), channel_id=1, source_target_pairs={{0,16},{4,12},{8,24},{12,4},{16,0},{20,28},{24,8},{28,20},{1,17},{... | collective-permute-start | bytes 786440 | tf_op jit(solution)/shard_map/ppermute | solution.py:33
  33.9 10.2 %collective-permute-start.10 = (bf16[512,256]{1,0:T(8,128)(2,1)S(1)}, bf16[512,256]{1,0:T(8,128)(2,1)S(1)}, u32[]{:S(2)}, u32[]{:S(2)}) collective-permute-start(bf16[512,256]{1,0:T(8,128)(2,1)S(1)} %add_add_fusion.refs_0_), channel_id=1, source_target_pairs={{0,4},{4,0},{8,12},{12,8},{16,20},{20,16},{24,28},{28,24},{1,5},{5... | collective-permute-start | bytes 786440 | tf_op jit(solution)/shard_map/ppermute | solution.py:23
  33.9 10.2 %collective-permute-start.12 = (bf16[512,256]{1,0:T(8,128)(2,1)S(1)}, bf16[512,256]{1,0:T(8,128)(2,1)S(1)}, u32[]{:S(2)}, u32[]{:S(2)}) collective-permute-start(bf16[512,256]{1,0:T(8,128)(2,1)S(1)} %collective-permute-done.11.refs_2_.refs_0_), channel_id=1, source_target_pairs={{0,4},{4,0},{8,12},{12,8},{16,20},{20,16},{24,28},{28,24},{1,5},{5... | collective-permute-start | bytes 786440 | tf_op jit(solution)/shard_map/ppermute | solution.py:23
  34.4 9.7 %collective-permute-start.14 = (bf16[512,256]{1,0:T(8,128)(2,1)S(1)}, bf16[512,256]{1,0:T(8,128)(2,1)S(1)}, u32[]{:S(2)}, u32[]{:S(2)}) collective-permute-start(bf16[512,256]{1,0:T(8,128)(2,1)S(1)} %collective-permute-done.13.refs_4_.refs_2_), channel_id=1, source_target_pairs={{0,4},{4,0},{8,12},{12,8},{16,20},{20,16},{24,28},{28,24},{1,5},{5... | collective-permute-start | bytes 786440 | tf_op jit(solution)/shard_map/ppermute | solution.py:23
  39.2 5.0 %collective-permute-start.16 = (bf16[512,256]{1,0:T(8,128)(2,1)}, bf16[512,256]{1,0:T(8,128)(2,1)}, u32[]{:S(2)}, u32[]{:S(2)}) collective-permute-start(bf16[512,256]{1,0:T(8,128)(2,1)} %collective-permute-done.15.refs_6_.refs_0_), channel_id=1, source_target_pairs={{0,4},{4,0},{8,12},{12,8},{16,20},{20,16},{24,28},{28,24},{1,5},{5... | collective-permute-start | bytes 786440 | tf_op jit(solution)/shard_map/ppermute | solution.py:23
  44.1 0.7 copy-start.18
  44.1 0.8 copy-start.19
  44.1 0.9 copy-start.20
  49.2 2.5 %collective-permute-start.18 = (bf16[2,256,512]{2,1,0:T(8,128)(2,1)}, bf16[2,256,512]{2,1,0:T(8,128)(2,1)S(1)}, u32[]{:S(2)}, u32[]{:S(2)}) collective-permute-start(bf16[2,256,512]{2,1,0:T(8,128)(2,1)} %products.3.refs_2_.refs_8_), channel_id=1, source_target_pairs={{0,4},{4,0},{8,12},{12,8},{16,20},{20,16},{24,28},{28,24},{1,5},{5... | collective-permute-start | bytes 1572872 | tf_op jit(solution)/shard_map/ppermute | solution.py:23
  49.7 14.0 %collective-permute-start.19 = (bf16[2,256,512]{2,1,0:T(8,128)(2,1)}, bf16[2,256,512]{2,1,0:T(8,128)(2,1)S(1)}, u32[]{:S(2)}, u32[]{:S(2)}) collective-permute-start(bf16[2,256,512]{2,1,0:T(8,128)(2,1)} %products.3.refs_2_.refs_8_), channel_id=1, source_target_pairs={{0,16},{4,20},{8,24},{12,28},{16,0},{20,4},{24,8},{28,12},{1,17},{... | collective-permute-start | bytes 1572872 | tf_op jit(solution)/shard_map/ppermute | solution.py:23
  50.9 13.8 %collective-permute-start.17 = (bf16[2,256,512]{2,1,0:T(8,128)(2,1)}, bf16[2,256,512]{2,1,0:T(8,128)(2,1)S(1)}, u32[]{:S(2)}, u32[]{:S(2)}) collective-permute-start(bf16[2,256,512]{2,1,0:T(8,128)(2,1)} %products.3.refs_2_.refs_8_), channel_id=1, source_target_pairs={{0,8},{4,12},{8,0},{12,4},{16,24},{20,28},{24,16},{28,20},{1,9},{5... | collective-permute-start | bytes 1572872 | tf_op jit(solution)/shard_map/ppermute | solution.py:23
  51.8 0.8 copy-start.4
  63.8 2.8 %copy-start = (bf16[2,256,512]{2,1,0:T(8,128)(2,1)}, bf16[2,256,512]{2,1,0:T(8,128)(2,1)S(1)}, u32[]{:S(2)}) copy-start(bf16[2,256,512]{2,1,0:T(8,128)(2,1)S(1)} %collective-permute-done.19.refs_6_.refs_8_.refs_12_) | copy-start | bytes 1572868
  63.8 2.7 %collective-permute-start.22 = (bf16[2,256,512]{2,1,0:T(8,128)(2,1)S(1)}, bf16[2,256,512]{2,1,0:T(8,128)(2,1)S(1)}, u32[]{:S(2)}, u32[]{:S(2)}) collective-permute-start(bf16[2,256,512]{2,1,0:T(8,128)(2,1)S(1)} %collective-permute-done.19.refs_6_.refs_8_.refs_12_), channel_id=1, source_target_pairs={{0,4},{4,0},{8,12},{12,8},{16,20},{20,16},{24,28},{28,24},{1,5},{5... | collective-permute-start | bytes 1572872 | tf_op jit(solution)/shard_map/ppermute | solution.py:23
  64.7 1.9 %copy-start.1 = (bf16[2,256,512]{2,1,0:T(8,128)(2,1)}, bf16[2,256,512]{2,1,0:T(8,128)(2,1)S(1)}, u32[]{:S(2)}) copy-start(bf16[2,256,512]{2,1,0:T(8,128)(2,1)S(1)} %collective-permute-done.17.refs_4_.refs_6_.refs_10_) | copy-start | bytes 1572868
  64.7 1.9 %collective-permute-start.21 = (bf16[2,256,512]{2,1,0:T(8,128)(2,1)S(1)}, bf16[2,256,512]{2,1,0:T(8,128)(2,1)S(1)}, u32[]{:S(2)}, u32[]{:S(2)}) collective-permute-start(bf16[2,256,512]{2,1,0:T(8,128)(2,1)S(1)} %collective-permute-done.17.refs_4_.refs_6_.refs_10_), channel_id=1, source_target_pairs={{0,4},{4,0},{8,12},{12,8},{16,20},{20,16},{24,28},{28,24},{1,5},{5... | collective-permute-start | bytes 1572872 | tf_op jit(solution)/shard_map/ppermute | solution.py:23
  65.6 9.4 %copy-start.10 = (bf16[2,256,512]{2,1,0:T(8,128)(2,1)S(1)}, bf16[2,256,512]{2,1,0:T(8,128)(2,1)}, u32[]{:S(2)}) copy-start(bf16[2,256,512]{2,1,0:T(8,128)(2,1)} %products.2.refs_8_) | copy-start | bytes 1572868
  65.6 9.4 %collective-permute-start.20 = (bf16[2,256,512]{2,1,0:T(8,128)(2,1)}, bf16[2,256,512]{2,1,0:T(8,128)(2,1)S(1)}, u32[]{:S(2)}, u32[]{:S(2)}) collective-permute-start(bf16[2,256,512]{2,1,0:T(8,128)(2,1)} %broadcast_select_fusion), channel_id=1, source_target_pairs={{0,16},{4,12},{8,24},{12,4},{16,0},{20,28},{24,8},{28,20},{1,17},{... | collective-permute-start | bytes 1572872 | tf_op jit(solution)/shard_map/ppermute | solution.py:33
  66.5 0.8 copy-start.2
  67.3 0.8 copy-start.3
  75.0 3.6 %copy-start.11 = (bf16[2,256,512]{2,1,0:T(8,128)(2,1)}, bf16[2,256,512]{2,1,0:T(8,128)(2,1)S(1)}, u32[]{:S(2)}) copy-start(bf16[2,256,512]{2,1,0:T(8,128)(2,1)S(1)} %collective-permute-done.20.refs_2_.refs_10_.refs_14_) | copy-start | bytes 1572868
  75.0 3.6 %collective-permute-start.25 = (bf16[2,256,512]{2,1,0:T(8,128)(2,1)S(1)}, bf16[2,256,512]{2,1,0:T(8,128)(2,1)S(1)}, u32[]{:S(2)}, u32[]{:S(2)}) collective-permute-start(bf16[2,256,512]{2,1,0:T(8,128)(2,1)S(1)} %collective-permute-done.20.refs_2_.refs_10_.refs_14_), channel_id=1, source_target_pairs={{0,4},{4,0},{8,12},{12,8},{16,20},{20,16},{24,28},{28,24},{1,5},{5... | collective-permute-start | bytes 1572872 | tf_op jit(solution)/shard_map/ppermute | solution.py:23
  75.0 32.2 %collective-permute-start.29 = (bf16[2,256,512]{2,1,0:T(8,128)(2,1)S(1)}, bf16[2,256,512]{2,1,0:T(8,128)(2,1)S(1)}, u32[]{:S(2)}, u32[]{:S(2)}) collective-permute-start(bf16[2,256,512]{2,1,0:T(8,128)(2,1)S(1)} %copy-done.10), channel_id=1, source_target_pairs={{0,24},{4,28},{8,16},{12,20},{16,8},{20,12},{24,0},{28,4},{1,25},{... | collective-permute-start | bytes 1572872 | tf_op jit(solution)/shard_map/ppermute | solution.py:23
  76.9 30.8 %collective-permute-start.27 = (bf16[2,256,512]{2,1,0:T(8,128)(2,1)S(1)}, bf16[2,256,512]{2,1,0:T(8,128)(2,1)S(1)}, u32[]{:S(2)}, u32[]{:S(2)}) collective-permute-start(bf16[2,256,512]{2,1,0:T(8,128)(2,1)S(1)} %copy-done.10), channel_id=1, source_target_pairs={{0,16},{4,20},{8,24},{12,28},{16,0},{20,4},{24,8},{28,12},{1,17},{... | collective-permute-start | bytes 1572872 | tf_op jit(solution)/shard_map/ppermute | solution.py:23
  77.6 30.2 %collective-permute-start.24 = (bf16[2,256,512]{2,1,0:T(8,128)(2,1)S(1)}, bf16[2,256,512]{2,1,0:T(8,128)(2,1)S(1)}, u32[]{:S(2)}, u32[]{:S(2)}) collective-permute-start(bf16[2,256,512]{2,1,0:T(8,128)(2,1)S(1)} %copy-done.10), channel_id=1, source_target_pairs={{0,8},{4,12},{8,0},{12,4},{16,24},{20,28},{24,16},{28,20},{1,9},{5... | collective-permute-start | bytes 1572872 | tf_op jit(solution)/shard_map/ppermute | solution.py:23
  78.6 48.8 %collective-permute-start.23 = (bf16[2,256,512]{2,1,0:T(8,128)(2,1)S(1)}, bf16[2,256,512]{2,1,0:T(8,128)(2,1)}, u32[]{:S(2)}, u32[]{:S(2)}) collective-permute-start(bf16[2,256,512]{2,1,0:T(8,128)(2,1)S(1)} %copy-done.10), channel_id=1, source_target_pairs={{0,4},{4,0},{8,12},{12,8},{16,20},{20,16},{24,28},{28,24},{1,5},{5... | collective-permute-start | bytes 1572872 | tf_op jit(solution)/shard_map/ppermute | solution.py:23
  78.6 0.8 copy-start.12
  107.2 9.4 %copy-start.21 = (bf16[2,256,512]{2,1,0:T(8,128)(2,1)}, bf16[2,256,512]{2,1,0:T(8,128)(2,1)S(1)}, u32[]{:S(2)}) copy-start(bf16[2,256,512]{2,1,0:T(8,128)(2,1)S(1)} %collective-permute-done.29.refs_14_) | copy-start | bytes 1572868
  107.2 20.1 %collective-permute-start.30 = (bf16[2,256,512]{2,1,0:T(8,128)(2,1)S(1)}, bf16[2,256,512]{2,1,0:T(8,128)(2,1)S(1)}, u32[]{:S(2)}, u32[]{:S(2)}) collective-permute-start(bf16[2,256,512]{2,1,0:T(8,128)(2,1)S(1)} %collective-permute-done.29.refs_14_), channel_id=1, source_target_pairs={{0,4},{4,0},{8,12},{12,8},{16,20},{20,16},{24,28},{28,24},{1,5},{5... | collective-permute-start | bytes 1572872 | tf_op jit(solution)/shard_map/ppermute | solution.py:23
  107.7 8.9 %copy-start.22 = (bf16[2,256,512]{2,1,0:T(8,128)(2,1)}, bf16[2,256,512]{2,1,0:T(8,128)(2,1)S(1)}, u32[]{:S(2)}) copy-start(bf16[2,256,512]{2,1,0:T(8,128)(2,1)S(1)} %collective-permute-done.27.refs_12_) | copy-start | bytes 1572868
  107.7 19.6 %collective-permute-start.28 = (bf16[2,256,512]{2,1,0:T(8,128)(2,1)S(1)}, bf16[2,256,512]{2,1,0:T(8,128)(2,1)S(1)}, u32[]{:S(2)}, u32[]{:S(2)}) collective-permute-start(bf16[2,256,512]{2,1,0:T(8,128)(2,1)S(1)} %collective-permute-done.27.refs_12_), channel_id=1, source_target_pairs={{0,4},{4,0},{8,12},{12,8},{16,20},{20,16},{24,28},{28,24},{1,5},{5... | collective-permute-start | bytes 1572872 | tf_op jit(solution)/shard_map/ppermute | solution.py:23
  107.8 8.8 %copy-start.23 = (bf16[2,256,512]{2,1,0:T(8,128)(2,1)}, bf16[2,256,512]{2,1,0:T(8,128)(2,1)S(1)}, u32[]{:S(2)}) copy-start(bf16[2,256,512]{2,1,0:T(8,128)(2,1)S(1)} %collective-permute-done.24.refs_10_) | copy-start | bytes 1572868
  107.8 19.6 %collective-permute-start.26 = (bf16[2,256,512]{2,1,0:T(8,128)(2,1)S(1)}, bf16[2,256,512]{2,1,0:T(8,128)(2,1)}, u32[]{:S(2)}, u32[]{:S(2)}) collective-permute-start(bf16[2,256,512]{2,1,0:T(8,128)(2,1)S(1)} %collective-permute-done.24.refs_10_), channel_id=1, source_target_pairs={{0,4},{4,0},{8,12},{12,8},{16,20},{20,16},{24,28},{28,24},{1,5},{5... | collective-permute-start | bytes 1572872 | tf_op jit(solution)/shard_map/ppermute | solution.py:23
  127.4 0.9 copy-start.24
  127.4 1.0 copy-start.25
